TPU v7x, 128 devices: a whole 4x4x4 slice. The times are simulated.
128 devices in a mesh: dom: 32 (over z, x, core), sub: 4 (over y).
Axes of the slice: x: 4, y: 4, z: 4, core: 2. Of those that a mesh axis runs over, the one named last changes fastest.
Arguments:
- position: float32 [3, 524288], P(None, ('dom', 'sub')), may hold values from -3 to 3
- smoothing: float32 [524288], P(('dom', 'sub')), may hold values from 0.7 to 1.4
- mass: float32 [524288], P(('dom', 'sub')), may hold values from 0.001 to 0.004
- energy: float32 [524288], P(('dom', 'sub')), may hold values from 0.5 to 2
- species: float32 [12, 524288], P(None, ('dom', 'sub')), may hold values from 0 to 1
- neighbours: int32 [4096, 4], P(('dom', 'sub')), may hold values from 0 to 31
- exports: int32 [1024, 2], P(('dom', 'sub')), may hold values from 0 to 31
- imports: int32 [2048, 2], P(('dom', 'sub')), may hold values from 0 to 31
- jac_inverse: float32 [12, 12], replicated
- rates: float32 [12, 12], replicated, may hold values from -1.75 to 1.75
- chem_steps: int32 [524288], P(('dom', 'sub')), may hold values from 1 to 32, as said below
- dense_slot: int32 [524288], P(('dom', 'sub')), may hold values from -1 to 2559, as said below
Outputs:
- density: float32 [524288], P(('dom', 'sub'))
- accel: float32 [3, 524288], P(None, ('dom', 'sub'))
- abundances: float32 [12, 524288], P(None, ('dom', 'sub'))
Inputs may be any that keep to these rules, and one draw needn't show every extreme that they name: chem_steps is above 4 exactly on particles with dense_slot >= 0, at most 4 elsewhere. `dense_slot`: A value s below 1280 names slot s of this device's dense-clump buffer; 1280 + s names slot s of the buffer of the next device along dom (the last wraps to the first, same sub index). No two particles name the same slot of the same buffer.
All inputs are finite; a program needn't handle non-finite values.
Results may differ from a plain program's by a relative error of at most 0.0003.
Values sent between devices are 32-bit elements; how exact they have to be, the bound alone decides.
A program may use at most 64 MiB of HBM per device.

v0:
```python
import jax
import jax.numpy as jnp
from jax import lax
from jax.sharding import PartitionSpec as P

BLOCK = 128
SPECIES = 12
S_LO = 4
SMAX = 32
RCAP = 1280


gamma_gas = 5.0 / 3.0
chem_tau = 0.5
map_batch = 16


def extended(cells, sides, width):
    for axis, dim in sides:
        count = lax.axis_size(axis)
        head = lax.slice_in_dim(cells, 0, width, axis=dim)
        tail = lax.slice_in_dim(cells, cells.shape[dim] - width, cells.shape[dim], axis=dim)
        cells = jnp.concatenate(
            [
                lax.ppermute(tail, axis, [(i, (i + 1) % count) for i in range(count)]),
                cells,
                lax.ppermute(head, axis, [((i + 1) % count, i) for i in range(count)]),
            ],
            axis=dim,
        )
    return cells


def pair_kernel(
    tgt_pos, tgt_width, src_pos, src_mass, src_factor, with_density, with_first, with_second
):
    offset = tgt_pos[:, :, None] - src_pos[:, None, :]
    squared = jnp.sum(offset * offset, axis=0)
    inv_sq = 1.0 / (tgt_width * tgt_width)
    base = 1.0 / (1.0 + squared * inv_sq[:, None])
    pieces = []
    if with_density:
        dens = jnp.sum(base * base * src_mass[None, :], axis=1) / (
            tgt_width * tgt_width * tgt_width
        )
        pieces.append(dens[None, :])
    if with_first or with_second:
        slope = (-4.0 * inv_sq * inv_sq / tgt_width)[:, None] * base * base * base
        weighted = slope * src_mass[None, :]
        pieces.append(jnp.sum(offset * weighted[None], axis=2))
        pieces.append(jnp.sum(offset * (weighted * src_factor[None, :])[None], axis=2))
    return jnp.concatenate(pieces, axis=0)


def group_terms(tgt_fields, tgt_rows, src_fields, src_rows, flags):

    def single(record):
        target, sources = record
        picked = src_fields[:, sources]
        flat = picked.reshape(picked.shape[0], -1)
        return pair_kernel(
            tgt_fields[:3, target],
            tgt_fields[3, target],
            flat[:3],
            flat[3],
            flat[4],
            flags[0],
            flags[1],
            flags[2],
        )

    return lax.map(single, (tgt_rows, src_rows), batch_size=map_batch)


def chem_update(abund, drive_gain, jac_inverse, rates):
    drive = (
        jnp.tanh(
            jnp.dot(
                rates, abund, precision=lax.Precision.HIGHEST, preferred_element_type=jnp.float32
            )
        )
        + 1.0
    )
    return jnp.dot(
        jac_inverse,
        abund + chem_tau * drive_gain[None, :] * drive,
        precision=lax.Precision.HIGHEST,
        preferred_element_type=jnp.float32,
    )


def dense_cycles(buffer, jac_inverse, rates):
    abund = buffer[:SPECIES]
    drive_gain = buffer[SPECIES]
    limit = buffer[SPECIES + 1]

    def advance(cycle_no, current):
        update = chem_update(current, drive_gain, jac_inverse, rates)
        return jnp.where((cycle_no.astype(jnp.float32) < limit)[None, :], update, current)

    return lax.fori_loop(S_LO, SMAX, advance, abund)


def add_owned(owner_map, returned):
    return jnp.einsum("bg,gck->bck", owner_map, returned, precision=lax.Precision.HIGHEST)


def peer_swap(payload):
    moved = lax.all_to_all(payload, "sub", split_axis=1, concat_axis=1, tiled=True)
    padded = extended(moved, (("dom", 0),), 1)
    result = jnp.concatenate([padded[0:1], padded[3:4]], 0)
    return result


def on_device(
    position,
    smoothing,
    mass,
    energy,
    species,
    neighbours,
    exports,
    imports,
    jac_inverse,
    rates,
    chem_steps,
    dense_slot,
):
    blocks = neighbours.shape[0]
    slots = exports.shape[1]
    sub_count = lax.axis_size("sub")
    chosen = exports.reshape(-1)
    outgoing = chosen.shape[0]
    tgt_fields = jnp.concatenate([position, smoothing[None]], 0).reshape(4, blocks, BLOCK)
    blockwise = jnp.transpose(tgt_fields, (1, 0, 2))
    packed = blockwise[chosen].reshape(2, sub_count, slots, 4, BLOCK)
    arrived = peer_swap(packed).reshape(outgoing, 4, BLOCK)
    arrived_fields = jnp.transpose(arrived, (1, 0, 2))
    first_flags = (True, False, False)
    later_flags = (False, True, True)
    all_rows = jnp.arange(blocks, dtype=jnp.int32)
    import_rows = jnp.arange(outgoing, dtype=jnp.int32)
    owner_map = (chosen[None, :] == all_rows[:, None]).astype(jnp.float32)
    zero_field = jnp.zeros_like(mass)
    src_first = jnp.concatenate([position, mass[None], zero_field[None]], 0).reshape(
        5, blocks, BLOCK
    )
    local_one = group_terms(tgt_fields, all_rows, src_first, neighbours, first_flags)
    remote_one = group_terms(arrived_fields, import_rows, src_first, imports, first_flags)
    width_one = remote_one.shape[1]
    returned_one = peer_swap(remote_one.reshape(2, sub_count, slots, width_one, BLOCK))
    summed_one = local_one + add_owned(owner_map, returned_one.reshape(outgoing, width_one, BLOCK))
    density = summed_one[:, 0].reshape(-1)
    factor = (gamma_gas - 1.0) * energy / density
    src_second = jnp.concatenate([position, mass[None], factor[None]], 0).reshape(5, blocks, BLOCK)
    local_two = group_terms(tgt_fields, all_rows, src_second, neighbours, later_flags)
    remote_two = group_terms(arrived_fields, import_rows, src_second, imports, later_flags)
    width_two = remote_two.shape[1]
    returned_two = peer_swap(remote_two.reshape(2, sub_count, slots, width_two, BLOCK))
    summed_two = local_two + add_owned(owner_map, returned_two.reshape(outgoing, width_two, BLOCK))
    first = summed_two[:, 0:3]
    second = summed_two[:, 3:6]
    first = jnp.transpose(first, (1, 0, 2)).reshape(3, -1)
    second = jnp.transpose(second, (1, 0, 2)).reshape(3, -1)
    accel = -(factor[None, :] * first + second)
    drive_gain = density / (density + 1.0)
    abund = species
    for cycle_no in range(S_LO):
        update = chem_update(abund, drive_gain, jac_inverse, rates)
        abund = jnp.where((cycle_no < chem_steps)[None, :], update, abund)
    values = jnp.concatenate([abund, drive_gain[None], chem_steps.astype(jnp.float32)[None]], 0)
    channels = SPECIES + 2
    local_index = jnp.where(dense_slot >= 0, dense_slot, 2 * RCAP)
    buffer = (
        jnp.zeros((channels, 2 * RCAP), jnp.float32).at[:, local_index].add(values, mode="drop")
    )
    finished = dense_cycles(buffer, jac_inverse, rates)
    settled = finished[:, jnp.clip(dense_slot, 0, 2 * RCAP - 1)]
    abund = jnp.where((dense_slot >= 0)[None, :], settled, abund)
    return (density, accel, abund)


def solution(mesh):
    placed = (
        P(None, ("dom", "sub")),
        P(("dom", "sub")),
        P(("dom", "sub")),
        P(("dom", "sub")),
        P(None, ("dom", "sub")),
        P(("dom", "sub"), None),
        P(("dom", "sub"), None),
        P(("dom", "sub"), None),
        P(),
        P(),
        P(("dom", "sub")),
        P(("dom", "sub")),
    )
    return jax.shard_map(
        on_device,
        mesh=mesh,
        in_specs=placed,
        out_specs=(P(("dom", "sub")), P(None, ("dom", "sub")), P(None, ("dom", "sub"))),
        check_vma=False,
    )
```

profile of v0, /device:TPU:0, one launch (start us, length us, event | category | flops | bytes accessed | tf_op | source)
XLA Modules:
  0.0 169.4 jit_solution(6832604725167041077)
XLA Ops:
  0.6 0.8 copy.184
  1.5 0.9 fusion.79
  3.6 4.6 %all-to-all-start = ((f32[2,4,2,4,128]{4,3,2,0,1:T(4,128)}), f32[2,4,2,4,128]{4,3,2,0,1:T(4,128)S(1)}, u32[]{:S(2)}, u32[]{:S(2)}) async-start(f32[2,4,2,4,128]{4,3,2,0,1:T(4,128)} %copy.186), calls=%async_computation | async-start | bytes 65536 | tf_op jit(solution)/shard_map/all_to_all | solution.py:109
  8.2 0.9 pad_maximum_fusion.1
  9.1 0.8 reshape.409
  9.9 0.9 fusion.39
  10.9 11.9 %while.11 = (s32[]{:T(128)}, f32[2,16,1,128]{3,1,2,0:T(8,128)S(1)}, s32[2,16]{1,0:T(2,128)S(1)}, f32[4,32,128]{2,1,0:T(8,128)S(1)}, s32[2,16,4]{1,2,0:T(4,128)S(1)}, /*index=5*/f32[5,32,128]{2,0,1:T(8,128)S(1)}, s32[]{:T(128)}) while((s32[]{:T(128)}, f32[2,16,1,128]{3,1,2,0:T(8,128)S(1)}, s32[2,16]{1,0:T(2,128)S(1)}, ...), condition=%wide.region_3.4_spmd, body=%wide.region_0.3_spmd.sunk | while | flops 14689570 | bytes 10164897 | solution.py:72
  11.5 0.7 gather_fusion.1
  12.4 0.6 gather_fusion.2
  13.3 2.2 %multiply_reduce_fusion.8 = f32[16,128,512]{2,1,0:T(8,128)S(1)} fusion(f32[16,3,128]{2,1,0:T(4,128)S(1)} %copy.238, f32[16,3,512]{2,1,0:T(4,128)S(1)} %copy.241), kind=kLoop, calls=%fused_computation.13.clone.1 | loop fusion | flops 8388608 | bytes 4317184 | tf_op jit(solution)/shard_map/while/body/eval_jaxpr/vmap()/reduce_sum | solution.py:38
  15.5 1.3 multiply_reduce_fusion.9
  17.5 0.7 gather_fusion.1
  19.2 2.2 %multiply_reduce_fusion.8 = f32[16,128,512]{2,1,0:T(8,128)S(1)} fusion(f32[16,3,128]{2,1,0:T(4,128)S(1)} %copy.238, f32[16,3,512]{2,1,0:T(4,128)S(1)} %copy.241), kind=kLoop, calls=%fused_computation.13.clone.1 | loop fusion | flops 8388608 | bytes 4317184 | tf_op jit(solution)/shard_map/while/body/eval_jaxpr/vmap()/reduce_sum | solution.py:38
  21.4 1.3 multiply_reduce_fusion.9
  23.8 5.5 %collective-permute-start.1 = (f32[1,4,2,4,128]{4,3,2,0,1:T(4,128)S(1)}, f32[1,4,2,4,128]{4,3,2,0,1:T(4,128)S(1)}, u32[]{:S(2)}, u32[]{:S(2)}) collective-permute-start(f32[1,4,2,4,128]{4,3,2,0,1:T(4,128)S(1)} %get-tuple-element.402), channel_id=1, source_target_pairs={{4,0},{8,4},{12,8},{16,12},{20,16},{24,20},{28,24},{32,28},{36,32}... | collective-permute-start | bytes 49160 | tf_op jit(solution)/shard_map/ppermute | solution.py:27
  29.3 1.4 collective-permute-done.1
  30.7 5.0 %collective-permute-done = f32[1,4,2,4,128]{4,3,2,0,1:T(4,128)S(1)} collective-permute-done((f32[1,4,2,4,128]{4,3,2,0,1:T(4,128)S(1)}, f32[1,4,2,4,128]{4,3,2,0,1:T(4,128)S(1)}, u32[]{:S(2)}, u32[]{:S(2)}) %collective-permute-start) | collective-permute-done | bytes 16416 | tf_op jit(solution)/shard_map/ppermute | solution.py:25
  35.8 0.6 gather_fusion.7
  37.1 1.2 multiply_reduce_fusion.3
  38.3 0.8 multiply_reduce_fusion.4
  39.6 4.5 %all-to-all-start.1 = ((f32[2,4,2,1,128]{4,2,0,3,1:T(2,128)}), f32[2,4,2,1,128]{4,2,0,3,1:T(2,128)S(1)}, u32[]{:S(2)}, u32[]{:S(2)}) async-start(f32[2,4,2,1,128]{4,2,0,3,1:T(2,128)} %copy.192), calls=%async_computation.1 | async-start | bytes 16384 | tf_op jit(solution)/shard_map/all_to_all | solution.py:109
  44.2 5.3 %all-to-all-done.1 = f32[2,4,2,1,128]{4,2,0,3,1:T(2,128)S(1)} async-done(((f32[2,4,2,1,128]{4,2,0,3,1:T(2,128)}), f32[2,4,2,1,128]{4,2,0,3,1:T(2,128)S(1)}, u32[]{:S(2)}, u32[]{:S(2)}) %all-to-all-start.1) | async-done | bytes 8224 | tf_op jit(solution)/shard_map/all_to_all | solution.py:109
  50.1 0.7 collective-permute-done.3
  50.8 5.1 %collective-permute-done.2 = f32[1,4,2,1,128]{4,2,0,3,1:T(2,128)S(1)} collective-permute-done((f32[1,4,2,1,128]{4,2,0,3,1:T(2,128)S(1)}, f32[1,4,2,1,128]{4,2,0,3,1:T(2,128)S(1)}, u32[]{:S(2)}, u32[]{:S(2)}) %collective-permute-start.2) | collective-permute-done | bytes 4128 | tf_op jit(solution)/shard_map/ppermute | solution.py:25
  57.1 1.2 fusion.13
  58.3 0.8 broadcast_multiply_fusion.1
  59.1 3.0 %fusion.14 = (f32[16,3,128]{2,1,0:T(4,128)S(1)}, f32[16,3,128]{2,1,0:T(4,128)S(1)}) fusion(f32[16,3,128]{2,1,0:T(4,128)S(1)} %copy.188, f32[16,128,256]{2,1,0:T(8,128)S(1)} %get-tuple-element.388, f32[16,3,256]{2,1,0:T(4,128)S(1)} %copy.198, f32[16,128,256]{2,1,0:T(8,128)S(1)} %get-tuple-element.387), kind=kLoop, calls=%fused_computation.64 | loop fusion | flops 7852032 | bytes 4317184 | tf_op jit(solution)/shard_map/while/body/eval_jaxpr/vmap()/reduce_sum | solution.py:50
  62.1 0.6 copy.200
  62.8 3.5 %all-to-all-start.2 = ((f32[2,4,2,6,128]{4,2,0,3,1:T(2,128)}), f32[2,4,2,6,128]{4,2,0,3,1:T(2,128)S(1)}, u32[]{:S(2)}, u32[]{:S(2)}) async-start(f32[2,4,2,6,128]{4,2,0,3,1:T(2,128)} %copy.200), calls=%async_computation.2 | async-start | bytes 98304 | tf_op jit(solution)/shard_map/all_to_all | solution.py:109
  69.4 2.0 %copy.202 = f32[4096,14]{1,0:T(8,128)} copy(f32[4096,14]{0,1:T(8,128)S(1)} %maximum_bitcast_fusion.1) | data formatting | bytes 458752 | tf_op jit(solution)/shard_map/concatenate | solution.py:171
  71.3 23.0 %scatter_custom_fusion = f32[14,2560]{0,1:T(8,128)S(1)} fusion(s32[4096]{0:T(1024)S(1)} %get-tuple-element.404, f32[4096,14]{1,0:T(8,128)} %copy.202, f32[]{:T(128)} %constant.105.clone.1), kind=kCustom, calls=%fused_computation.101 | custom fusion | flops 57344 | bytes 143872 | tf_op jit(solution)/shard_map/scatter-add | solution.py:175
  94.3 1.1 fusion.53
  96.2 19.8 %while.43 = (s32[]{:T(128)}, f32[12,2560]{1,0:T(8,128)S(1)}, f32[2560]{0:T(1024)S(1)}, f32[1,2560]{1,0:T(1,128)S(1)}, f32[12,12]{1,0:T(8,128)S(1)}, /*index=5*/f32[12,12]{1,0:T(8,128)S(1)}, s32[]{:T(128)}, s32[]{:T(128)}) while((s32[]{:T(128)}, f32[12,2560]{1,0:T(8,128)S(1)}, f32[2560]{0:T(1024)S(1)}, f32[1,2560]{1,0:T(1,128)S(1)}, ...), condition=%wide.region_16.17_spmd, body=%wide.region_15.16_spmd.sunk | while | flops 8975364 | bytes 661749 | solution.py:101
  116.0 28.7 %while.42 = (s32[]{:T(128)}, f32[2,16,6,128]{3,1,0,2:T(8,128)S(1)}, s32[2,16]{1,0:T(2,128)S(1)}, f32[4,32,128]{2,1,0:T(8,128)S(1)}, s32[2,16,4]{1,2,0:T(4,128)S(1)}, /*index=5*/f32[5,32,128]{2,0,1:T(8,128)S(1)}, s32[]{:T(128)}) while((s32[]{:T(128)}, f32[2,16,6,128]{3,1,0,2:T(8,128)S(1)}, s32[2,16]{1,0:T(2,128)S(1)}, ...), condition=%wide.region_10.11_spmd, body=%wide.region_6.10_spmd.sunk | while | flops 32517408 | bytes 27409056 | solution.py:72
  116.1 0.7 gather_fusion.3
  117.8 4.1 %fusion.91 = f32[16,128,512]{2,1,0:T(8,128)} fusion(f32[16,3,128]{2,1,0:T(4,128)S(1)} %copy.243, f32[16,3,512]{2,1,0:T(4,128)S(1)} %copy.246), kind=kLoop, calls=%fused_computation.31.clone.1 | loop fusion | flops 8388608 | bytes 4317184 | tf_op jit(solution)/shard_map/while/body/eval_jaxpr/vmap()/reduce_sum | solution.py:38
  122.6 3.1 %broadcast_multiply_fusion.3 = (f32[16,128,512]{2,1,0:T(8,128)S(1)}, f32[16,128,512]{2,1,0:T(8,128)S(1)}) fusion(f32[16,512]{1,0:T(8,128)S(1)} %get-tuple-element.535, f32[16,512]{1,0:T(8,128)S(1)} %get-tuple-element.536, f32[16,128,512]{2,1,0:T(8,128)} %fusion.91, f32[16,128]{1,0:T(8,128)S(1)} %get-tuple-element.538, ...), kind=kLoop, calls=%fused_computation.36.clone.1 | loop fusion | flops 8388608 | bytes 12664832 | tf_op jit(solution)/shard_map/while/body/eval_jaxpr/vmap()/mul | solution.py:51
  125.6 4.7 %fusion.93 = (f32[16,3,128]{2,1,0:T(4,128)S(1)}, f32[16,3,128]{2,1,0:T(4,128)S(1)}) fusion(f32[16,3,128]{2,1,0:T(4,128)S(1)} %copy.243, f32[16,128,512]{2,1,0:T(8,128)S(1)} %get-tuple-element.540, f32[16,3,512]{2,1,0:T(4,128)S(1)} %copy.246, f32[16,128,512]{2,1,0:T(8,128)S(1)} %get-tuple-element.541), kind=kLoop, calls=%fused_computation.32.clone.1 | loop fusion | flops 15716352 | bytes 8560640 | tf_op jit(solution)/shard_map/while/body/eval_jaxpr/vmap()/reduce_sum | solution.py:50
  130.4 0.7 gather_fusion.3
  131.3 0.6 gather_fusion.4
  132.2 4.1 %fusion.91 = f32[16,128,512]{2,1,0:T(8,128)} fusion(f32[16,3,128]{2,1,0:T(4,128)S(1)} %copy.243, f32[16,3,512]{2,1,0:T(4,128)S(1)} %copy.246), kind=kLoop, calls=%fused_computation.31.clone.1 | loop fusion | flops 8388608 | bytes 4317184 | tf_op jit(solution)/shard_map/while/body/eval_jaxpr/vmap()/reduce_sum | solution.py:38
  136.9 3.1 %broadcast_multiply_fusion.3 = (f32[16,128,512]{2,1,0:T(8,128)S(1)}, f32[16,128,512]{2,1,0:T(8,128)S(1)}) fusion(f32[16,512]{1,0:T(8,128)S(1)} %get-tuple-element.535, f32[16,512]{1,0:T(8,128)S(1)} %get-tuple-element.536, f32[16,128,512]{2,1,0:T(8,128)} %fusion.91, f32[16,128]{1,0:T(8,128)S(1)} %get-tuple-element.538, ...), kind=kLoop, calls=%fused_computation.36.clone.1 | loop fusion | flops 8388608 | bytes 12664832 | tf_op jit(solution)/shard_map/while/body/eval_jaxpr/vmap()/mul | solution.py:51
  140.0 4.7 %fusion.93 = (f32[16,3,128]{2,1,0:T(4,128)S(1)}, f32[16,3,128]{2,1,0:T(4,128)S(1)}) fusion(f32[16,3,128]{2,1,0:T(4,128)S(1)} %copy.243, f32[16,128,512]{2,1,0:T(8,128)S(1)} %get-tuple-element.540, f32[16,3,512]{2,1,0:T(4,128)S(1)} %copy.246, f32[16,128,512]{2,1,0:T(8,128)S(1)} %get-tuple-element.541), kind=kLoop, calls=%fused_computation.32.clone.1 | loop fusion | flops 15716352 | bytes 8560640 | tf_op jit(solution)/shard_map/while/body/eval_jaxpr/vmap()/reduce_sum | solution.py:50
  145.2 14.2 %gather_fusion.11 = f32[4096,12]{1,0:T(8,128)} fusion(f32[12,2560]{0,1:T(8,128)S(1)} %copy.205, s32[4096]{0:T(1024)S(1)} %get-tuple-element.403), kind=kCustom, calls=%fused_computation.11 | custom fusion | bytes 409600 | tf_op jit(solution)/shard_map/gather | solution.py:178
  159.3 2.2 %copy.206 = f32[4096,12]{0,1:T(8,128)S(1)} copy(f32[4096,12]{1,0:T(8,128)} %gather_fusion.11) | data formatting | bytes 393216 | tf_op jit(solution)/shard_map/gather | solution.py:178
  162.2 0.7 bitcast_select_fusion
  163.2 5.1 %collective-permute-done.4 = f32[1,4,2,6,128]{4,2,0,3,1:T(2,128)S(1)} collective-permute-done((f32[1,4,2,6,128]{4,2,0,3,1:T(2,128)S(1)}, f32[1,4,2,6,128]{4,2,0,3,1:T(2,128)S(1)}, u32[]{:S(2)}, u32[]{:S(2)}) %collective-permute-start.4) | collective-permute-done | bytes 24608 | tf_op jit(solution)/shard_map/ppermute | solution.py:25
  168.7 0.7 fusion.40
  (267 shorter events, 34.8 us)
Async XLA Ops:
  3.6 20.2 %all-to-all-start = ((f32[2,4,2,4,128]{4,3,2,0,1:T(4,128)}), f32[2,4,2,4,128]{4,3,2,0,1:T(4,128)S(1)}, u32[]{:S(2)}, u32[]{:S(2)}) async-start(f32[2,4,2,4,128]{4,3,2,0,1:T(4,128)} %copy.186), calls=%async_computation | async-start | bytes 65536 | tf_op jit(solution)/shard_map/all_to_all | solution.py:109
  10.9 11.9 %copy-start.9 = (s32[16,2]{0,1:T(2,128)S(1)}, s32[16,2]{0,1:T(2,128)}, u32[]{:S(2)}) copy-start(s32[16,2]{0,1:T(2,128)} %param.25) | copy-start | bytes 388
  10.9 12.9 %copy-start.5 = (s32[4096]{0:T(1024)S(1)}, s32[4096]{0:T(1024)}, u32[]{:S(2)}) copy-start(s32[4096]{0:T(1024)} %param.29) | copy-start | bytes 49156
  22.8 21.4 %copy-start.6 = (s32[4096]{0:T(1024)S(1)}, s32[4096]{0:T(1024)}, u32[]{:S(2)}) copy-start(s32[4096]{0:T(1024)} %param.28) | copy-start | bytes 49156
  22.8 33.4 %copy-start.8 = (f32[4096]{0:T(1024)S(1)}, f32[4096]{0:T(1024)}, u32[]{:S(2)}) copy-start(f32[4096]{0:T(1024)} %param.21) | copy-start | bytes 49156
  22.8 33.5 %copy-start.1 = (f32[3,4096]{1,0:T(4,128)S(1)}, f32[3,4096]{1,0:T(4,128)}, u32[]{:S(2)}) copy-start(f32[3,4096]{1,0:T(4,128)} %param.18) | copy-start | bytes 147460
  22.8 33.5 %copy-start.4 = (f32[4096]{0:T(1024)S(1)}, f32[4096]{0:T(1024)}, u32[]{:S(2)}) copy-start(f32[4096]{0:T(1024)} %param.20) | copy-start | bytes 49156
  23.8 6.9 %collective-permute-start.1 = (f32[1,4,2,4,128]{4,3,2,0,1:T(4,128)S(1)}, f32[1,4,2,4,128]{4,3,2,0,1:T(4,128)S(1)}, u32[]{:S(2)}, u32[]{:S(2)}) collective-permute-start(f32[1,4,2,4,128]{4,3,2,0,1:T(4,128)S(1)} %get-tuple-element.402), channel_id=1, source_target_pairs={{4,0},{8,4},{12,8},{16,12},{20,16},{24,20},{28,24},{32,28},{36,32}... | collective-permute-start | bytes 49160 | tf_op jit(solution)/shard_map/ppermute | solution.py:27
  29.3 6.5 %collective-permute-start = (f32[1,4,2,4,128]{4,3,2,0,1:T(4,128)S(1)}, f32[1,4,2,4,128]{4,3,2,0,1:T(4,128)S(1)}, u32[]{:S(2)}, u32[]{:S(2)}) collective-permute-start(f32[1,4,2,4,128]{4,3,2,0,1:T(4,128)S(1)} %get-tuple-element.401), channel_id=1, source_target_pairs={{0,4},{4,8},{8,12},{12,16},{16,20},{20,24},{24,28},{28,32},{32,36}... | collective-permute-start | bytes 49160 | tf_op jit(solution)/shard_map/ppermute | solution.py:25
  39.6 9.8 %all-to-all-start.1 = ((f32[2,4,2,1,128]{4,2,0,3,1:T(2,128)}), f32[2,4,2,1,128]{4,2,0,3,1:T(2,128)S(1)}, u32[]{:S(2)}, u32[]{:S(2)}) async-start(f32[2,4,2,1,128]{4,2,0,3,1:T(2,128)} %copy.192), calls=%async_computation.1 | async-start | bytes 16384 | tf_op jit(solution)/shard_map/all_to_all | solution.py:109
  49.5 1.3 collective-permute-start.3
  49.5 6.4 %collective-permute-start.2 = (f32[1,4,2,1,128]{4,2,0,3,1:T(2,128)S(1)}, f32[1,4,2,1,128]{4,2,0,3,1:T(2,128)S(1)}, u32[]{:S(2)}, u32[]{:S(2)}) collective-permute-start(f32[1,4,2,1,128]{4,2,0,3,1:T(2,128)S(1)} %get-tuple-element.413), channel_id=1, source_target_pairs={{0,4},{4,8},{8,12},{12,16},{16,20},{20,24},{24,28},{28,32},{32,36}... | collective-permute-start | bytes 12296 | tf_op jit(solution)/shard_map/ppermute | solution.py:25
  56.2 12.7 %copy-start.7 = (f32[32,128]{1,0:T(8,128)}, f32[32,128]{1,0:T(8,128)S(1)}, u32[]{:S(2)}) copy-start(f32[32,128]{1,0:T(8,128)S(1)} %convolution_add_fusion.1) | copy-start | bytes 49156
  58.3 8.0 %copy-start = (f32[12,4096]{1,0:T(8,128)S(1)}, f32[12,4096]{1,0:T(8,128)}, u32[]{:S(2)}) copy-start(f32[12,4096]{1,0:T(8,128)} %param.22) | copy-start | bytes 589828
  58.3 8.0 %copy-start.3 = (f32[12,12]{1,0:T(8,128)S(1)}, f32[12,12]{1,0:T(8,128)}, u32[]{:S(2)}) copy-start(f32[12,12]{1,0:T(8,128)} %param.27) | copy-start | bytes 1732
  59.1 7.5 %copy-start.2 = (f32[12,12]{1,0:T(8,128)S(1)}, f32[12,12]{1,0:T(8,128)}, u32[]{:S(2)}) copy-start(f32[12,12]{1,0:T(8,128)} %param.26) | copy-start | bytes 1732
  62.8 98.8 %all-to-all-start.2 = ((f32[2,4,2,6,128]{4,2,0,3,1:T(2,128)}), f32[2,4,2,6,128]{4,2,0,3,1:T(2,128)S(1)}, u32[]{:S(2)}, u32[]{:S(2)}) async-start(f32[2,4,2,6,128]{4,2,0,3,1:T(2,128)} %copy.200), calls=%async_computation.2 | async-start | bytes 98304 | tf_op jit(solution)/shard_map/all_to_all | solution.py:109
  161.6 1.6 collective-permute-start.5
  161.7 6.6 %collective-permute-start.4 = (f32[1,4,2,6,128]{4,2,0,3,1:T(2,128)S(1)}, f32[1,4,2,6,128]{4,2,0,3,1:T(2,128)S(1)}, u32[]{:S(2)}, u32[]{:S(2)}) collective-permute-start(f32[1,4,2,6,128]{4,2,0,3,1:T(2,128)S(1)} %get-tuple-element.399), channel_id=1, source_target_pairs={{0,4},{4,8},{8,12},{12,16},{16,20},{20,24},{24,28},{28,32},{32,36}... | collective-permute-start | bytes 73736 | tf_op jit(solution)/shard_map/ppermute | solution.py:25
where the time goes:
time: 170 us; the launch traced here: 169 us
  other arithmetic  66.2 us (39%)
  local copies, waits for them, and re-layouts  37.2 us (22%)
  waiting for transfers between devices  22.9 us (13%)
  matrix products  20.9 us (12%)
  starting transfers between devices  19.1 us (11%)
  loops' own time  1.88 us (1%)
    scatter-add x1, other arithmetic, on_device(): jnp.zeros((channels, 2 * RCAP), jnp.float32).at[:, local_index]  23 us
    gather x2, local copies, waits for them, and re-layouts, on_device(): settled = finished[:, jnp.clip(dense_slot, 0, 2 * RCAP - 1)]  16.4 us
    ppermute x3, waiting for transfers between devices, extended(): lax.ppermute(tail, axis, [(i, (i + 1) % count) for i in range(count)])  15.3 us
    reduce_sum x6, other arithmetic, pair_kernel(): squared = jnp.sum(offset * offset, axis=0)  14.9 us
    all_to_all x3, starting transfers between devices, peer_swap(): lax.all_to_all(payload, 'sub', split_axis=1, concat_axis=1, tiled=True)  12.5 us
    reduce_sum x3, other arithmetic, pair_kernel(): pieces.append(jnp.sum(offset * weighted[None], axis=2))  12.4 us
    dot_general x32, matrix products, chem_update(): jnp.dot(jac_inverse, abund + chem_tau * drive_gain[None, :] * drive, prec...  10.6 us
    dot_general x32, matrix products, chem_update(): jnp.dot(rates, abund, precision=lax.Precision.HIGHEST, preferred_element_...  9.69 us
  transfers between devices with their start and end apart: 9, of which 7 were waited for; matrix products, arithmetic and copies ran while one was open for 65% of the time, Pallas kernels for 0%

commit v1 on v0

v1 whole, which is shorter than its diff:
```python
import functools

import jax
import jax.numpy as jnp
from jax import lax
from jax.experimental import pallas as pl
from jax.experimental.pallas import tpu as pltpu
from jax.sharding import PartitionSpec as P

BLOCK = 128
BLOCKS = 32
NBR = 4
SLOTS = 16
SPECIES = 12
S_LO = 4
SMAX = 32
HALF = BLOCKS * BLOCK // 2
FEAT = 48
GROUPS = 4
MESH = pl.DeviceIdType.MESH
F32 = jnp.float32
BF16 = jnp.bfloat16
HIGH = lax.Precision.HIGHEST

gamma_gas = 5.0 / 3.0
chem_tau = 0.5


def pieces(value):
    high = value.astype(BF16).astype(F32)
    rest = value - high
    middle = rest.astype(BF16).astype(F32)
    return high, middle, rest - middle


def halves(value):
    high = value.astype(BF16)
    return high, (value - high.astype(F32)).astype(BF16)


def mm(a, b):
    return jnp.dot(a, b, preferred_element_type=F32)


def source_features(fields):
    high, middle, low = pieces(fields)
    return jnp.concatenate([high, high, high, middle, middle, low], 0).T.astype(BF16)


def gradient_rows(fields, factor):
    row = lax.broadcasted_iota(jnp.int32, fields.shape, 0)
    both = jnp.where(row < 4, fields, pltpu.roll(fields, 4, 0))
    high, low = halves(both * jnp.where(row < 4, 1.0, factor))
    return jnp.concatenate([high, low], 0)


def pair_terms(features, target, high_ref, low_ref):
    base = 1.0 / mm(features, target)
    squared = base * base
    high, low = halves(squared * base)
    high_ref[...] = high
    low_ref[...] = low
    return jnp.sum(squared, axis=0, keepdims=True)


def spread(matrix):
    wide = 2 * SPECIES
    pick = (
        lax.broadcasted_iota(jnp.int32, (wide, SPECIES), 0) % SPECIES
        == lax.broadcasted_iota(jnp.int32, (wide, SPECIES), 1)
    ).astype(F32)
    tall = jnp.dot(pick, matrix, precision=HIGH, preferred_element_type=F32)
    full = lax.dot_general(
        tall, pick, (((1,), (1,)), ((), ())), precision=HIGH, preferred_element_type=F32
    )
    same = (
        lax.broadcasted_iota(jnp.int32, (wide, wide), 0) // SPECIES
        == lax.broadcasted_iota(jnp.int32, (wide, wide), 1) // SPECIES
    )
    return jnp.where(same, full, 0.0)


def left_side(matrix):
    high, low = halves(matrix)
    return jnp.concatenate([high.astype(F32), high.astype(F32), low.astype(F32)], 1).astype(BF16)


def right_side(state):
    high, low = halves(state)
    return jnp.concatenate([high, low, high], 0)


def kernel(
    pos,
    width,
    mass,
    energy,
    species,
    neigh,
    exports,
    imports,
    jac,
    rates,
    steps,
    slot,
    dens_out,
    accel_out,
    abund_out,
    fields,
    targets,
    feats,
    far_feats,
    stage,
    far_fields,
    factor,
    stage_factor,
    far_factor,
    rows,
    far_rows,
    near_high,
    near_low,
    far_high,
    far_low,
    near_dens,
    far_dens,
    near_acc,
    far_acc,
    root_mass,
    gain,
    limit,
    state,
    rate_in,
    send_one,
    recv_one,
    send_two,
    recv_two,
):
    dom = lax.axis_index("dom")
    sub = lax.axis_index("sub")
    doms = lax.axis_size("dom")
    subs = lax.axis_size("sub")
    sides = [lax.rem(dom + doms - 1, doms), lax.rem(dom + 1, doms)]
    barrier = pltpu.get_barrier_semaphore()
    for side in sides:
        for q in range(subs):
            pl.semaphore_signal(barrier, inc=1, device_id=(side, q), device_id_type=MESH)

    def exchange(sent, landed, send_sem, recv_sem):
        copies = []
        for e in range(2):
            for q in range(subs):
                copies.append(
                    pltpu.make_async_remote_copy(
                        src_ref=sent.at[e * subs + q],
                        dst_ref=landed.at[(1 - e) * subs + sub],
                        send_sem=send_sem.at[e * subs + q],
                        recv_sem=recv_sem.at[(1 - e) * subs + sub],
                        device_id=(sides[e], q),
                        device_id_type=MESH,
                    )
                )
        return copies

    def arrive(sent, landed, send_sem, recv_sem):
        for e in range(2):
            for q in range(subs):
                pltpu.make_async_remote_copy(
                    src_ref=sent.at[e * subs + q],
                    dst_ref=landed.at[e * subs + q],
                    send_sem=send_sem.at[e * subs + q],
                    recv_sem=recv_sem.at[e * subs + q],
                    device_id=(sides[e], q),
                    device_id_type=MESH,
                ).wait_recv()

    root_mass[...] = 1.0 / jnp.sqrt(mass[...])

    def prepare(b, _):
        place = pos[:, pl.ds(pl.multiple_of(b * BLOCK, BLOCK), BLOCK)]
        weight = root_mass[pl.ds(b, 1)]
        norm = jnp.sum(place * place, axis=0, keepdims=True)
        fields[b, 0:3] = place * weight
        fields[b, 3:4] = weight
        fields[b, 4:5] = norm * weight
        fields[b, 5:8] = jnp.zeros((3, BLOCK), F32)
        span = width[pl.ds(b, 1)]
        target = jnp.concatenate(
            [place * -2.0, span * span + norm, jnp.ones_like(norm), jnp.zeros((3, BLOCK), F32)], 0
        )
        high, middle, low = pieces(target)
        targets[b] = jnp.concatenate([high, middle, low, high, middle, high], 0).astype(BF16)
        return 0

    lax.fori_loop(0, BLOCKS, prepare, 0, unroll=4)
    for r in range(SLOTS):
        for k in range(2):
            stage[r // 2, (r % 2) * 2 + k] = fields[imports[k, r]]
    jac_full = spread(jac[...])
    rate_full = spread(rates[...])
    both = jnp.dot(rate_full, jac_full, precision=HIGH, preferred_element_type=F32)
    left = left_side(jnp.concatenate([jac_full, both], 0))
    left_first = left_side(rate_full)
    pl.semaphore_wait(barrier, 2 * subs)
    first = exchange(stage, far_fields, send_one, recv_one)
    for copy in first:
        copy.start()

    def transposed(b, _):
        feats[b] = source_features(fields[b])
        return 0

    lax.fori_loop(0, BLOCKS, transposed, 0, unroll=4)

    def near_first(b, _):
        lhs = jnp.concatenate([feats[neigh[k, b]] for k in range(NBR)], 0)
        near_dens[pl.ds(b, 1)] = pair_terms(lhs, targets[b], near_high.at[b], near_low.at[b])
        return 0

    lax.fori_loop(0, BLOCKS, near_first, 0, unroll=4)
    arrive(stage, far_fields, send_one, recv_one)

    def far_transposed(j, _):
        for k in range(4):
            far_feats[j * 4 + k] = source_features(far_fields[j, k])
        return 0

    lax.fori_loop(0, SLOTS // 2, far_transposed, 0)

    def far_first(r, _):
        lhs = jnp.concatenate([far_feats[r * 2 + k] for k in range(2)], 0)
        target = targets[exports[lax.rem(r, 2), r // 2]]
        far_dens[pl.ds(r, 1)] = pair_terms(lhs, target, far_high.at[r], far_low.at[r])
        return 0

    lax.fori_loop(0, SLOTS, far_first, 0, unroll=4)

    owner = lax.broadcasted_iota(jnp.int32, (BLOCKS, BLOCK), 0)
    total = near_dens[...]
    for r in range(SLOTS):
        total += jnp.where(owner == exports[r % 2, r // 2], far_dens[r : r + 1], 0.0)
    density = total * width[...]
    dens_out[...] = density
    factor[...] = (gamma_gas - 1.0) * energy[...] / density
    for r in range(SLOTS):
        for k in range(2):
            stage_factor[r // 2, pl.ds((r % 2) * 2 + k, 1)] = factor[pl.ds(imports[k, r], 1)]
    gain_all = chem_tau * (density / (density + 1.0))
    most = jnp.where(slot[...] >= 0, steps[...], jnp.minimum(steps[...], S_LO)).astype(F32)
    second = exchange(stage_factor, far_factor, send_two, recv_two)
    for copy in second:
        copy.start()

    def rows_near(b, _):
        rows[b] = gradient_rows(fields[b], factor[pl.ds(b, 1)])
        return 0

    lax.fori_loop(0, BLOCKS, rows_near, 0, unroll=4)

    def near_second(b, _):
        lhs = jnp.concatenate([rows[neigh[k, b]] for k in range(NBR)], 1)
        out = mm(lhs, near_high[b]) + mm(lhs, near_low[b])
        near_acc[b] = out[0:8] + out[8:16]
        return 0

    lax.fori_loop(0, BLOCKS, near_second, 0, unroll=4)

    for b in range(BLOCKS // 2):
        for h in range(2):
            block = b + h * (BLOCKS // 2)
            at = pl.ds(b * BLOCK, BLOCK)
            span = pl.ds(h * SPECIES, SPECIES)
            gain[span, at] = jnp.broadcast_to(gain_all[block : block + 1], (SPECIES, BLOCK))
            limit[span, at] = jnp.broadcast_to(most[block : block + 1], (SPECIES, BLOCK))
    state[0:SPECIES] = species[:, 0:HALF]
    state[SPECIES : 2 * SPECIES] = species[:, HALF : 2 * HALF]
    part = HALF // GROUPS
    for g in range(GROUPS):
        at = pl.ds(g * part, part)
        rate_in[:, at] = mm(left_first, right_side(state[:, at]))

    def cycle(c, _):
        for g in range(GROUPS):
            at = pl.ds(g * part, part)
            abund = state[:, at]
            lift = gain[:, at]
            moved = (abund + lift) + lift * jnp.tanh(rate_in[:, at])
            out = mm(left, right_side(moved))
            rate_in[:, at] = out[2 * SPECIES :]
            state[:, at] = jnp.where(c.astype(F32) < limit[:, at], out[: 2 * SPECIES], abund)
        return 0

    lax.fori_loop(0, SMAX, cycle, 0, unroll=4)
    abund_out[:, 0:HALF] = state[0:SPECIES]
    abund_out[:, HALF : 2 * HALF] = state[SPECIES : 2 * SPECIES]

    arrive(stage_factor, far_factor, send_two, recv_two)

    def rows_far(j, _):
        for k in range(4):
            far_rows[j * 4 + k] = gradient_rows(far_fields[j, k], far_factor[j, pl.ds(k, 1)])
        return 0

    lax.fori_loop(0, SLOTS // 2, rows_far, 0)

    def far_second(r, _):
        lhs = jnp.concatenate([far_rows[r * 2 + k] for k in range(2)], 1)
        out = mm(lhs, far_high[r]) + mm(lhs, far_low[r])
        far_acc[r] = out[0:8] + out[8:16]
        return 0

    lax.fori_loop(0, SLOTS, far_second, 0, unroll=4)

    row = lax.broadcasted_iota(jnp.int32, (8, BLOCK), 0)

    def finish(b, _):
        acc = near_acc[b]
        for r in range(SLOTS):
            acc += far_acc[r] * (exports[r % 2, r // 2] == b).astype(F32)
        acc = acc * jnp.where(row < 4, factor[pl.ds(b, 1)], 1.0)
        acc = acc + pltpu.roll(acc, 4, 0)
        at = pl.ds(pl.multiple_of(b * BLOCK, BLOCK), BLOCK)
        accel_out[:, at] = (4.0 * width[pl.ds(b, 1)]) * (pos[:, at] * acc[3:4] - acc[0:3])
        return 0

    lax.fori_loop(0, BLOCKS, finish, 0, unroll=2)
    for copy in first + second:
        copy.wait_send()


def on_device(
    position,
    smoothing,
    mass,
    energy,
    species,
    neighbours,
    exports,
    imports,
    jac_inverse,
    rates,
    chem_steps,
    dense_slot,
):
    tile = (BLOCKS, BLOCK)
    vmem = pl.BlockSpec(memory_space=pltpu.VMEM)
    smem = pl.BlockSpec(memory_space=pltpu.SMEM)
    far = 2 * SLOTS
    density, accel, abund = pl.pallas_call(
        kernel,
        out_shape=(
            jax.ShapeDtypeStruct(tile, F32),
            jax.ShapeDtypeStruct(position.shape, F32),
            jax.ShapeDtypeStruct(species.shape, F32),
        ),
        in_specs=[vmem] * 5 + [smem] * 3 + [vmem] * 4,
        out_specs=(vmem, vmem, vmem),
        scratch_shapes=[
            pltpu.VMEM((BLOCKS, 8, BLOCK), F32),
            pltpu.VMEM((BLOCKS, FEAT, BLOCK), BF16),
            pltpu.VMEM((BLOCKS, BLOCK, FEAT), BF16),
            pltpu.VMEM((far, BLOCK, FEAT), BF16),
            pltpu.VMEM((SLOTS // 2, 4, 8, BLOCK), F32),
            pltpu.VMEM((SLOTS // 2, 4, 8, BLOCK), F32),
            pltpu.VMEM(tile, F32),
            pltpu.VMEM((SLOTS // 2, 4, BLOCK), F32),
            pltpu.VMEM((SLOTS // 2, 4, BLOCK), F32),
            pltpu.VMEM((BLOCKS, 16, BLOCK), BF16),
            pltpu.VMEM((far, 16, BLOCK), BF16),
            pltpu.VMEM((BLOCKS, NBR * BLOCK, BLOCK), BF16),
            pltpu.VMEM((BLOCKS, NBR * BLOCK, BLOCK), BF16),
            pltpu.VMEM((SLOTS, 2 * BLOCK, BLOCK), BF16),
            pltpu.VMEM((SLOTS, 2 * BLOCK, BLOCK), BF16),
            pltpu.VMEM(tile, F32),
            pltpu.VMEM((SLOTS, BLOCK), F32),
            pltpu.VMEM((BLOCKS, 8, BLOCK), F32),
            pltpu.VMEM((SLOTS, 8, BLOCK), F32),
            pltpu.VMEM(tile, F32),
            pltpu.VMEM((2 * SPECIES, HALF), F32),
            pltpu.VMEM((2 * SPECIES, HALF), F32),
            pltpu.VMEM((2 * SPECIES, HALF), F32),
            pltpu.VMEM((2 * SPECIES, HALF), F32),
            pltpu.SemaphoreType.DMA((SLOTS // 2,)),
            pltpu.SemaphoreType.DMA((SLOTS // 2,)),
            pltpu.SemaphoreType.DMA((SLOTS // 2,)),
            pltpu.SemaphoreType.DMA((SLOTS // 2,)),
        ],
        compiler_params=pltpu.CompilerParams(
            collective_id=0, has_side_effects=True, vmem_limit_bytes=67043328
        ),
        name="particle_step",
    )(
        position,
        smoothing.reshape(tile),
        mass.reshape(tile),
        energy.reshape(tile),
        species,
        neighbours.T,
        exports.T,
        imports.T,
        jac_inverse,
        rates,
        chem_steps.reshape(tile),
        dense_slot.reshape(tile),
    )
    return density.reshape(-1), accel, abund


def solution(mesh):
    flat = P(("dom", "sub"))
    wide = P(None, ("dom", "sub"))
    tall = P(("dom", "sub"), None)
    return jax.shard_map(
        on_device,
        mesh=mesh,
        in_specs=(wide, flat, flat, flat, wide, tall, tall, tall, P(), P(), flat, flat),
        out_specs=(flat, wide, wide),
        check_vma=False,
    )
```

time: 170 us -> 32.3 us (0.19)
  other arithmetic: 66.2 us -> 0 us
  local copies, waits for them, and re-layouts: 37.2 us -> 4.47 us
  Pallas kernels: 0 us -> 26.9 us
  waiting for transfers between devices: 22.9 us -> 0 us
  matrix products: 20.9 us -> 0 us
  starting transfers between devices: 19.1 us -> 0 us
  loops' own time: 1.88 us -> 0 us
    reduce_sum x12 -> x0, other arithmetic: 30.6 us -> none  [the longest x6 14.9 us: pair_kernel(): squared = jnp.sum(offset * offset, axis=0)]
    gather x30 -> x0, local copies, waits for them, and re-layouts: 27.4 us -> none  [the longest x2 16.4 us: on_device(): settled = finished[:, jnp.clip(dense_slot, 0, 2 * RCAP - 1)]]
    pallas_call x0 -> x1, Pallas kernels: none -> 26.9 us  [on_device(): pl.pallas_call(kernel, out_shape=(jax.ShapeDtypeStruct(tile, F32), jax.Sh...]
    scatter-add x1 -> x0, other arithmetic: 23 us -> none  [on_device(): jnp.zeros((channels, 2 * RCAP), jnp.float32).at[:, local_index]]
    dot_general x66 -> x0, matrix products: 20.9 us -> none  [the longest x32 10.6 us: chem_update(): jnp.dot(jac_inverse, abund + chem_tau * drive_gain[None, :] * drive, prec...]
    ppermute x6 -> x0, waiting for transfers between devices: 17.6 us -> none  [the longest x3 15.3 us: extended(): lax.ppermute(tail, axis, [(i, (i + 1) % count) for i in range(count)])]
    all_to_all x3 -> x0, starting transfers between devices: 12.5 us -> none  [peer_swap(): lax.all_to_all(payload, 'sub', split_axis=1, concat_axis=1, tiled=True)]
    mul x32 -> x0, other arithmetic: 7.83 us -> none  [the longest x3 6.91 us: pair_kernel(): weighted * src_factor[None, :]]
  transfers between devices with their start and end apart: 9 -> 0, of which waited for: 7 -> 0; matrix products, arithmetic and copies ran while one was open for 65% -> 0% of each run, Pallas kernels for 0% -> 0%
where the time goes in v1:
time: 32.3 us; the launch traced here: 32 us
  Pallas kernels  26.9 us (83%)
  local copies, waits for them, and re-layouts  4.47 us (14%)
  between operations  0.64 us (2%)
    pallas_call x1, Pallas kernels, on_device(): pl.pallas_call(kernel, out_shape=(jax.ShapeDtypeStruct(tile, F32), jax.Sh...  26.9 us
    unnamed x3, local copies, waits for them, and re-layouts  4.47 us

profile of v1, /device:TPU:0, one launch (start us, length us, event | category | flops | bytes accessed | tf_op | source)
XLA Modules:
  0.0 32.0 jit_solution(11284917587231312849)
XLA Ops:
  0.6 26.9 %particle_step.1 = (f32[32,128]{1,0:T(8,128)}, f32[3,4096]{1,0:T(4,128)}, f32[12,4096]{1,0:T(8,128)}) custom-call(f32[3,4096]{1,0:T(4,128)} %pos.1, f32[32,128]{1,0:T(8,128)} %bitcast.10, f32[32,128]{1,0:T(8,128)} %bitcast.11, f32[32,128]{1,0:T(8,128)} %bitcast.12, f32[12,4096]{1,0:T(8,128)} %species.1, s32[4,32]{1,0:T(4,128)} %bitcast.15, s32[2,8]{1,0:T(2,128)} %bitcast.16, ...), custom_call_target="tpu_custom_call" | custom-call | tf_op jit(solution)/shard_map/particle_step/pallas_call | solution.py:348
  27.5 1.3 %copy.18 = f32[4096]{0:T(1024)} copy(f32[4096]{0:T(1024)} %bitcast.9) | data formatting | bytes 32768
  28.9 1.5 %copy.19 = f32[3,4096]{1,0:T(4,128)} copy(f32[3,4096]{1,0:T(4,128)} %get-tuple-element.13) | data formatting | bytes 98304
  30.3 1.7 %copy.20 = f32[12,4096]{1,0:T(8,128)} copy(f32[12,4096]{1,0:T(8,128)} %get-tuple-element.14) | data formatting | bytes 393216

commit v2 on v1

v2 whole, which is shorter than its diff:
```python
import functools

import jax
import jax.numpy as jnp
from jax import lax
from jax.experimental import pallas as pl
from jax.experimental.pallas import tpu as pltpu
from jax.sharding import PartitionSpec as P

BLOCK = 128
BLOCKS = 32
NBR = 4
SLOTS = 16
SPECIES = 12
S_LO = 4
SMAX = 32
HALF = BLOCKS * BLOCK // 2
FEAT = 48
GROUPS = 4
FIRST = 8
MESH = pl.DeviceIdType.MESH
F32 = jnp.float32
BF16 = jnp.bfloat16
HIGH = lax.Precision.HIGHEST

gamma_gas = 5.0 / 3.0
chem_tau = 0.5


def pieces(value):
    high = value.astype(BF16).astype(F32)
    rest = value - high
    middle = rest.astype(BF16).astype(F32)
    return high, middle, rest - middle


def halves(value):
    high = value.astype(BF16)
    return high, (value - high.astype(F32)).astype(BF16)


def mm(a, b):
    return jnp.dot(a, b, preferred_element_type=F32)


def source_features(fields):
    high, middle, low = pieces(fields)
    return jnp.concatenate([high, high, high, middle, middle, low], 0).T.astype(BF16)


def gradient_rows(fields, factor):
    row = lax.broadcasted_iota(jnp.int32, fields.shape, 0)
    both = jnp.where(row < 4, fields, pltpu.roll(fields, 4, 0))
    high, low = halves(both * jnp.where(row < 4, 1.0, factor))
    return jnp.concatenate([high, low], 0)


def pair_terms(features, target, cubes, dens, row):
    total = None
    for k, feature in enumerate(features):
        base = 1.0 / mm(feature, target)
        squared = base * base
        cubes[k * BLOCK : (k + 1) * BLOCK] = squared * base
        part = jnp.sum(squared.reshape(BLOCK // 8, 8, BLOCK), axis=0)
        total = part if total is None else total + part
    dens[pl.ds(row, 1)] = jnp.sum(total, axis=0, keepdims=True)


def pair_sums(rows, cubes):
    high, low = halves(cubes[...])
    lhs = jnp.concatenate(rows, 1)
    out = mm(lhs, high) + mm(lhs, low)
    return out[0:8] + out[8:16]


def spread(matrix):
    wide = 2 * SPECIES
    pick = (
        lax.broadcasted_iota(jnp.int32, (wide, SPECIES), 0) % SPECIES
        == lax.broadcasted_iota(jnp.int32, (wide, SPECIES), 1)
    ).astype(F32)
    tall = jnp.dot(pick, matrix, precision=HIGH, preferred_element_type=F32)
    full = lax.dot_general(
        tall, pick, (((1,), (1,)), ((), ())), precision=HIGH, preferred_element_type=F32
    )
    same = (
        lax.broadcasted_iota(jnp.int32, (wide, wide), 0) // SPECIES
        == lax.broadcasted_iota(jnp.int32, (wide, wide), 1) // SPECIES
    )
    return jnp.where(same, full, 0.0)


def left_side(matrix):
    high, low = halves(matrix)
    return jnp.concatenate([high.astype(F32), high.astype(F32), low.astype(F32)], 1).astype(BF16)


def right_side(state):
    high, low = halves(state)
    return jnp.concatenate([high, low, high], 0)


def kernel(
    pos_in,
    width_in,
    mass_in,
    energy_in,
    species_in,
    neigh_in,
    exports_in,
    imports_in,
    jac_in,
    rates_in,
    steps_in,
    slot_in,
    density,
    accel,
    abund_all,
    pos,
    width,
    mass,
    energy,
    species,
    neigh,
    exports,
    imports,
    jac,
    rates,
    steps,
    slot,
    fields,
    targets,
    feats,
    stage,
    far_fields,
    factor,
    stage_factor,
    far_factor,
    rows,
    far_rows,
    near_cubes,
    far_cubes,
    near_dens,
    far_dens,
    near_acc,
    far_acc,
    root_mass,
    gain,
    limit,
    state,
    rate_in,
    load_sem,
    send_one,
    recv_one,
    send_two,
    recv_two,
):
    dom = lax.axis_index("dom")
    sub = lax.axis_index("sub")
    doms = lax.axis_size("dom")
    subs = lax.axis_size("sub")
    sides = [lax.rem(dom + doms - 1, doms), lax.rem(dom + 1, doms)]
    barrier = pltpu.get_barrier_semaphore()
    for side in sides:
        for q in range(subs):
            pl.semaphore_signal(barrier, inc=1, device_id=(side, q), device_id_type=MESH)

    pairs = {
        "pos": (pos_in, pos),
        "mass": (mass_in, mass),
        "imports": (imports_in, imports),
        "width": (width_in, width),
        "neigh": (neigh_in, neigh),
        "exports": (exports_in, exports),
        "jac": (jac_in, jac),
        "rates": (rates_in, rates),
        "energy": (energy_in, energy),
        "steps": (steps_in, steps),
        "slot": (slot_in, slot),
        "species": (species_in, species),
    }
    loads = {}
    for i, (name, (source, target)) in enumerate(pairs.items()):
        loads[name] = pltpu.make_async_copy(source, target, load_sem.at[i])
        loads[name].start()

    def exchange(sent, landed, send_sem, recv_sem):
        copies = []
        for e in range(2):
            for q in range(subs):
                copies.append(
                    pltpu.make_async_remote_copy(
                        src_ref=sent.at[e * subs + q],
                        dst_ref=landed.at[(1 - e) * subs + sub],
                        send_sem=send_sem.at[e * subs + q],
                        recv_sem=recv_sem.at[(1 - e) * subs + sub],
                        device_id=(sides[e], q),
                        device_id_type=MESH,
                    )
                )
        return copies

    def arrive(place, sent, landed, send_sem, recv_sem):
        pltpu.make_async_remote_copy(
            src_ref=sent.at[place],
            dst_ref=landed.at[place],
            send_sem=send_sem.at[place],
            recv_sem=recv_sem.at[place],
            device_id=(sides[0], 0),
            device_id_type=MESH,
        ).wait_recv()

    loads["pos"].wait()
    loads["mass"].wait()
    root_mass[...] = 1.0 / jnp.sqrt(mass[...])

    def prepare(b, _):
        place = pos[:, pl.ds(pl.multiple_of(b * BLOCK, BLOCK), BLOCK)]
        weight = root_mass[pl.ds(b, 1)]
        fields[b, 0:3] = place * weight
        fields[b, 3:4] = weight
        fields[b, 4:5] = jnp.sum(place * place, axis=0, keepdims=True) * weight
        fields[b, 5:8] = jnp.zeros((3, BLOCK), F32)
        return 0

    lax.fori_loop(0, BLOCKS, prepare, 0, unroll=8)
    loads["imports"].wait()
    for r in range(SLOTS):
        for k in range(2):
            stage[r // 2, (r % 2) * 2 + k] = fields[imports[k, r]]
    loads["width"].wait()
    loads["neigh"].wait()
    loads["exports"].wait()
    loads["jac"].wait()
    loads["rates"].wait()
    pl.semaphore_wait(barrier, 2 * subs)
    first = exchange(stage, far_fields, send_one, recv_one)
    for copy in first:
        copy.start()

    def shape_block(b):
        place = pos[:, pl.ds(pl.multiple_of(b * BLOCK, BLOCK), BLOCK)]
        norm = jnp.sum(place * place, axis=0, keepdims=True)
        span = width[pl.ds(b, 1)]
        target = jnp.concatenate(
            [place * -2.0, span * span + norm, jnp.ones_like(norm), jnp.zeros((3, BLOCK), F32)], 0
        )
        high, middle, low = pieces(target)
        targets[b] = jnp.concatenate([high, middle, low, high, middle, high], 0).astype(BF16)
        feats[b] = source_features(fields[b])

    for b in range(FIRST):
        shape_block(b)
    jac_full = spread(jac[...])
    rate_full = spread(rates[...])
    both = jnp.dot(rate_full, jac_full, precision=HIGH, preferred_element_type=F32)
    left = left_side(jnp.concatenate([jac_full, both], 0))
    left_first = left_side(rate_full)

    def shape_more(b, _):
        shape_block(b)
        return 0

    lax.fori_loop(FIRST, BLOCKS, shape_more, 0, unroll=4)

    def near_first(b, _):
        parts = [feats[neigh[k, b]] for k in range(NBR)]
        pair_terms(parts, targets[b], near_cubes.at[b], near_dens, b)
        return 0

    lax.fori_loop(0, BLOCKS, near_first, 0, unroll=4)
    for name in ("energy", "steps", "slot", "species"):
        loads[name].wait()

    def far_first(i, _):
        q = lax.rem(sub + i + (i // 2) * (1 - 2 * lax.rem(i, 2)), subs)
        for e in range(2):
            arrive(e * subs + q, stage, far_fields, send_one, recv_one)
        for e in range(2):
            place = e * subs + q
            parts = [source_features(far_fields[place, k]) for k in range(4)]
            for x in range(2):
                slot_at = place * 2 + x
                target = targets[exports[x, place]]
                pair_terms(
                    parts[2 * x : 2 * x + 2], target, far_cubes.at[slot_at], far_dens, slot_at
                )
        return 0

    lax.fori_loop(0, subs, far_first, 0)

    owner = lax.broadcasted_iota(jnp.int32, (BLOCKS, BLOCK), 0)
    total = near_dens[...]
    for r in range(SLOTS):
        total += jnp.where(owner == exports[r % 2, r // 2], far_dens[r : r + 1], 0.0)
    dens = total * width[...]
    density[...] = dens
    factor[...] = (gamma_gas - 1.0) * energy[...] / dens
    for r in range(SLOTS):
        for k in range(2):
            stage_factor[r // 2, pl.ds((r % 2) * 2 + k, 1)] = factor[pl.ds(imports[k, r], 1)]
    gain_all = chem_tau * (dens / (dens + 1.0))
    most = jnp.where(slot[...] >= 0, steps[...], jnp.minimum(steps[...], S_LO)).astype(F32)
    for b in range(BLOCKS // 2):
        for h in range(2):
            block = b + h * (BLOCKS // 2)
            at = pl.ds(b * BLOCK, BLOCK)
            span = pl.ds(h * SPECIES, SPECIES)
            gain[span, at] = jnp.broadcast_to(gain_all[block : block + 1], (SPECIES, BLOCK))
            limit[span, at] = jnp.broadcast_to(most[block : block + 1], (SPECIES, BLOCK))
    state[0:SPECIES] = species[:, 0:HALF]
    state[SPECIES : 2 * SPECIES] = species[:, HALF : 2 * HALF]
    second = exchange(stage_factor, far_factor, send_two, recv_two)
    for copy in second:
        copy.start()
    part = HALF // GROUPS
    for g in range(GROUPS):
        at = pl.ds(g * part, part)
        rate_in[:, at] = mm(left_first, right_side(state[:, at]))

    def rows_near(b, _):
        rows[b] = gradient_rows(fields[b], factor[pl.ds(b, 1)])
        return 0

    lax.fori_loop(0, BLOCKS, rows_near, 0, unroll=8)

    def chem_step(c):
        for g in range(GROUPS):
            at = pl.ds(g * part, part)
            abund = state[:, at]
            lift = gain[:, at]
            moved = (abund + lift) + lift * jnp.tanh(rate_in[:, at])
            out = mm(left, right_side(moved))
            rate_in[:, at] = out[2 * SPECIES :]
            state[:, at] = jnp.where(c.astype(F32) < limit[:, at], out[: 2 * SPECIES], abund)

    def with_near(i, _):
        for s in range(4):
            chem_step(i * 4 + s)
            for n in range(2):
                b = i * 8 + s * 2 + n
                near_acc[b] = pair_sums([rows[neigh[k, b]] for k in range(NBR)], near_cubes.at[b])
        return 0

    lax.fori_loop(0, 4, with_near, 0)
    for place in range(2 * subs):
        arrive(place, stage_factor, far_factor, send_two, recv_two)
    for j in range(2 * subs):
        for k in range(4):
            far_rows[j * 4 + k] = gradient_rows(far_fields[j, k], far_factor[j, k : k + 1])

    def with_far(i, _):
        for s in range(4):
            chem_step(16 + i * 4 + s)
            for n in range(2):
                r = i * 8 + s * 2 + n
                far_acc[r] = pair_sums([far_rows[r * 2 + k] for k in range(2)], far_cubes.at[r])
        return 0

    lax.fori_loop(0, 2, with_far, 0)
    row = lax.broadcasted_iota(jnp.int32, (8, BLOCK), 0)

    def with_finish(i, _):
        for s in range(4):
            chem_step(24 + i * 4 + s)
            for n in range(4):
                b = i * 16 + s * 4 + n
                acc = near_acc[b]
                for r in range(SLOTS):
                    acc += far_acc[r] * (exports[r % 2, r // 2] == b).astype(F32)
                acc = acc * jnp.where(row < 4, factor[pl.ds(b, 1)], 1.0)
                acc = acc + pltpu.roll(acc, 4, 0)
                at = pl.ds(pl.multiple_of(b * BLOCK, BLOCK), BLOCK)
                accel[:, at] = (4.0 * width[pl.ds(b, 1)]) * (pos[:, at] * acc[3:4] - acc[0:3])
        return 0

    lax.fori_loop(0, 2, with_finish, 0)
    abund_all[:, 0:HALF] = state[0:SPECIES]
    abund_all[:, HALF : 2 * HALF] = state[SPECIES : 2 * SPECIES]
    for copy in first + second:
        copy.wait_send()


def deliver(density, accel, abund, dens_out, accel_out, abund_out, sems):
    pairs = ((abund, abund_out), (accel, accel_out), (density, dens_out))
    copies = [pltpu.make_async_copy(a, b, sems.at[i]) for i, (a, b) in enumerate(pairs)]
    for copy in copies:
        copy.start()
    for copy in copies:
        copy.wait()


def on_device(
    position,
    smoothing,
    mass,
    energy,
    species,
    neighbours,
    exports,
    imports,
    jac_inverse,
    rates,
    chem_steps,
    dense_slot,
):
    tile = (BLOCKS, BLOCK)
    vmem = pl.BlockSpec(memory_space=pltpu.VMEM)
    hbm = pl.BlockSpec(memory_space=pltpu.HBM)
    far = 2 * SLOTS
    sides = SLOTS // 2
    chem = (2 * SPECIES, HALF)
    given = (
        position,
        smoothing.reshape(tile),
        mass.reshape(tile),
        energy.reshape(tile),
        species,
        neighbours.T,
        exports.T,
        imports.T,
        jac_inverse,
        rates,
        chem_steps.reshape(tile),
        dense_slot.reshape(tile),
    )
    spaces = [pltpu.VMEM] * 5 + [pltpu.SMEM] * 3 + [pltpu.VMEM] * 4
    density, accel, abund = pl.pallas_call(
        kernel,
        out_shape=(
            pltpu.VMEM(tile, F32),
            pltpu.VMEM(position.shape, F32),
            pltpu.VMEM(species.shape, F32),
        ),
        in_specs=[hbm] * len(given),
        out_specs=(vmem, vmem, vmem),
        scratch_shapes=[space(x.shape, x.dtype) for space, x in zip(spaces, given)]
        + [
            pltpu.VMEM((BLOCKS, 8, BLOCK), F32),
            pltpu.VMEM((BLOCKS, FEAT, BLOCK), BF16),
            pltpu.VMEM((BLOCKS, BLOCK, FEAT), BF16),
            pltpu.VMEM((sides, 4, 8, BLOCK), F32),
            pltpu.VMEM((sides, 4, 8, BLOCK), F32),
            pltpu.VMEM(tile, F32),
            pltpu.VMEM((sides, 4, BLOCK), F32),
            pltpu.VMEM((sides, 4, BLOCK), F32),
            pltpu.VMEM((BLOCKS, 16, BLOCK), BF16),
            pltpu.VMEM((far, 16, BLOCK), BF16),
            pltpu.VMEM((BLOCKS, NBR * BLOCK, BLOCK), F32),
            pltpu.VMEM((SLOTS, 2 * BLOCK, BLOCK), F32),
            pltpu.VMEM(tile, F32),
            pltpu.VMEM((SLOTS, BLOCK), F32),
            pltpu.VMEM((BLOCKS, 8, BLOCK), F32),
            pltpu.VMEM((SLOTS, 8, BLOCK), F32),
            pltpu.VMEM(tile, F32),
            pltpu.VMEM(chem, F32),
            pltpu.VMEM(chem, F32),
            pltpu.VMEM(chem, F32),
            pltpu.VMEM(chem, F32),
            pltpu.SemaphoreType.DMA((len(given),)),
        ]
        + [pltpu.SemaphoreType.DMA((sides,))] * 4,
        compiler_params=pltpu.CompilerParams(
            collective_id=0, has_side_effects=True, vmem_limit_bytes=24 << 20
        ),
        name="particle_step",
    )(*(pltpu.with_memory_space_constraint(x, pltpu.HBM) for x in given))
    density, accel, abund = pl.pallas_call(
        deliver,
        out_shape=(
            jax.ShapeDtypeStruct(tile, F32),
            jax.ShapeDtypeStruct(position.shape, F32),
            jax.ShapeDtypeStruct(species.shape, F32),
        ),
        in_specs=[vmem] * 3,
        out_specs=(hbm,) * 3,
        scratch_shapes=[pltpu.SemaphoreType.DMA((3,))],
        compiler_params=pltpu.CompilerParams(vmem_limit_bytes=1 << 20),
        name="deliver",
    )(density, accel, abund)
    return density.reshape(-1), accel, abund


def solution(mesh):
    flat = P(("dom", "sub"))
    wide = P(None, ("dom", "sub"))
    tall = P(("dom", "sub"), None)
    return jax.shard_map(
        on_device,
        mesh=mesh,
        in_specs=(wide, flat, flat, flat, wide, tall, tall, tall, P(), P(), flat, flat),
        out_specs=(flat, wide, wide),
        check_vma=False,
    )
```

time: 32.3 us -> 25.3 us (0.78)
  local copies, waits for them, and re-layouts: 4.47 us -> 0 us
  Pallas kernels: 26.9 us -> 24.6 us
    unnamed x3 -> x0, local copies, waits for them, and re-layouts: 4.47 us -> none
    pallas_call x1 -> x2, Pallas kernels: 26.9 us -> 24.6 us  [the longest x1 23.8 us: on_device(): pl.pallas_call(kernel, out_shape=(pltpu.VMEM(tile, F32), pltpu.VMEM(posit...]
where the time goes in v2:
time: 25.3 us; the launch traced here: 25.2 us
  Pallas kernels  24.6 us (97%)
  between operations  0.64 us (3%)
    pallas_call x1, Pallas kernels, on_device(): pl.pallas_call(kernel, out_shape=(pltpu.VMEM(tile, F32), pltpu.VMEM(posit...  23.8 us
    pallas_call x1, Pallas kernels, on_device(): pl.pallas_call(deliver, out_shape=(jax.ShapeDtypeStruct(tile, F32), jax.S...  0.75 us

profile of v2, /device:TPU:0, one launch (start us, length us, event | category | flops | bytes accessed | tf_op | source)
XLA Modules:
  0.0 25.2 jit_solution(16740580389579662645)
XLA Ops:
  0.6 23.8 %particle_step.1 = (f32[32,128]{1,0:T(8,128)S(1)}, f32[3,4096]{1,0:T(4,128)S(1)}, f32[12,4096]{1,0:T(8,128)S(1)}) custom-call(f32[3,4096]{1,0:T(4,128)} %pos_in.1, f32[32,128]{1,0:T(8,128)} %bitcast.9, f32[32,128]{1,0:T(8,128)} %bitcast.10, f32[32,128]{1,0:T(8,128)} %bitcast.11, f32[12,4096]{1,0:T(8,128)} %species_in.1, s32[4,32]{1,0:T(4,128)} %bitcast.14, ...), custom_call_target="tpu_custom_call" | custom-call | tf_op jit(solution)/shard_map/particle_step/pallas_call | solution.py:428
  24.5 0.7 %deliver.1 = (f32[32,128]{1,0:T(8,128)}, f32[3,4096]{1,0:T(4,128)}, f32[12,4096]{1,0:T(8,128)}) custom-call(f32[32,128]{1,0:T(8,128)S(1)} %get-tuple-element.9.density, f32[3,4096]{1,0:T(4,128)S(1)} %get-tuple-element.10.accel, f32[12,4096]{1,0:T(8,128)S(1)} %get-tuple-element.11.abund), custom_call_target="tpu_custom_call" | custom-call | tf_op jit(solution)/shard_map/deliver/pallas_call | solution.py:468

commit v3 on v2

--- a/solution.py
+++ b/solution.py
@@ -55,14 +55,21 @@
     return jnp.concatenate([high, low], 0)
 
 
-def pair_terms(features, target, cubes, dens, row):
+def distances(features, target, place):
+    for k in range(0, len(features), 2):
+        place[k // 2] = mm(jnp.concatenate(features[k : k + 2], 1), target)
+
+
+def pair_terms(place, count, cubes, dens, row):
     total = None
-    for k, feature in enumerate(features):
-        base = 1.0 / mm(feature, target)
-        squared = base * base
-        cubes[k * BLOCK : (k + 1) * BLOCK] = squared * base
-        part = jnp.sum(squared.reshape(BLOCK // 8, 8, BLOCK), axis=0)
-        total = part if total is None else total + part
+    for k in range(count):
+        for half in range(2):
+            base = 1.0 / place[k, :, half * BLOCK : (half + 1) * BLOCK]
+            squared = base * base
+            at = (2 * k + half) * BLOCK
+            cubes[at : at + BLOCK] = squared * base
+            part = jnp.sum(squared.reshape(BLOCK // 8, 8, BLOCK), axis=0)
+            total = part if total is None else total + part
     dens[pl.ds(row, 1)] = jnp.sum(total, axis=0, keepdims=True)
 
 
@@ -75,14 +82,8 @@
 
 def spread(matrix):
     wide = 2 * SPECIES
-    pick = (
-        lax.broadcasted_iota(jnp.int32, (wide, SPECIES), 0) % SPECIES
-        == lax.broadcasted_iota(jnp.int32, (wide, SPECIES), 1)
-    ).astype(F32)
-    tall = jnp.dot(pick, matrix, precision=HIGH, preferred_element_type=F32)
-    full = lax.dot_general(
-        tall, pick, (((1,), (1,)), ((), ())), precision=HIGH, preferred_element_type=F32
-    )
+    tall = jnp.concatenate([matrix, matrix], 0)
+    full = jnp.concatenate([tall, tall], 1)
     same = (
         lax.broadcasted_iota(jnp.int32, (wide, wide), 0) // SPECIES
         == lax.broadcasted_iota(jnp.int32, (wide, wide), 1) // SPECIES
@@ -92,11 +93,13 @@
 
 def left_side(matrix):
     high, low = halves(matrix)
-    return jnp.concatenate([high.astype(F32), high.astype(F32), low.astype(F32)], 1).astype(BF16)
+    blank = jnp.zeros((matrix.shape[0], 8), F32)
+    high, low = high.astype(F32), low.astype(F32)
+    return jnp.concatenate([high, blank, high, blank, low, blank], 1).astype(BF16)
 
 
 def right_side(state):
-    high, low = halves(state)
+    high, low = halves(jnp.concatenate([state, jnp.zeros((8, state.shape[1]), F32)], 0))
     return jnp.concatenate([high, low, high], 0)
 
 
@@ -131,6 +134,9 @@
     fields,
     targets,
     feats,
+    far_feats,
+    even,
+    odd,
     stage,
     far_fields,
     factor,
@@ -210,6 +216,9 @@
             device_id_type=MESH,
         ).wait_recv()
 
+    feats[...] = jnp.zeros_like(feats)
+    targets[...] = jnp.zeros_like(targets)
+    far_feats[...] = jnp.zeros_like(far_feats)
     loads["pos"].wait()
     loads["mass"].wait()
     root_mass[...] = 1.0 / jnp.sqrt(mass[...])
@@ -246,15 +255,17 @@
             [place * -2.0, span * span + norm, jnp.ones_like(norm), jnp.zeros((3, BLOCK), F32)], 0
         )
         high, middle, low = pieces(target)
-        targets[b] = jnp.concatenate([high, middle, low, high, middle, high], 0).astype(BF16)
-        feats[b] = source_features(fields[b])
+        split = jnp.concatenate([high, middle, low, high, middle, high], 0).astype(BF16)
+        targets[b, 0:FEAT, 0:BLOCK] = split
+        targets[b, BLOCK : BLOCK + FEAT, BLOCK : 2 * BLOCK] = split
+        feats[b, :, 0:FEAT] = source_features(fields[b])
 
     for b in range(FIRST):
         shape_block(b)
     jac_full = spread(jac[...])
     rate_full = spread(rates[...])
-    both = jnp.dot(rate_full, jac_full, precision=HIGH, preferred_element_type=F32)
-    left = left_side(jnp.concatenate([jac_full, both], 0))
+    both = jnp.dot(rates[...], jac[...], precision=HIGH, preferred_element_type=F32)
+    left = left_side(jnp.concatenate([spread(both), jac_full], 0))
     left_first = left_side(rate_full)
 
     def shape_more(b, _):
@@ -263,31 +274,56 @@
 
     lax.fori_loop(FIRST, BLOCKS, shape_more, 0, unroll=4)
 
-    def near_first(b, _):
-        parts = [feats[neigh[k, b]] for k in range(NBR)]
-        pair_terms(parts, targets[b], near_cubes.at[b], near_dens, b)
+    def fill(b, place):
+        distances([feats[neigh[k, b]] for k in range(NBR)], targets[b], place)
+
+    def drain(b, place):
+        pair_terms(place, NBR // 2, near_cubes.at[b], near_dens, b)
+
+    fill(0, even.at[0])
+    fill(1, even.at[1])
+
+    def near_first(i, _):
+        b = i * 4
+        for n in range(2):
+            fill(b + 2 + n, odd.at[n])
+            drain(b + n, even.at[n])
+        for n in range(2):
+            fill(lax.rem(b + 4 + n, BLOCKS), even.at[n])
+            drain(b + 2 + n, odd.at[n])
         return 0
 
-    lax.fori_loop(0, BLOCKS, near_first, 0, unroll=4)
+    lax.fori_loop(0, BLOCKS // 4, near_first, 0)
     for name in ("energy", "steps", "slot", "species"):
         loads[name].wait()
 
-    def far_first(i, _):
-        q = lax.rem(sub + i + (i // 2) * (1 - 2 * lax.rem(i, 2)), subs)
+    def far_fill(i, place):
+        q = lax.rem(sub + (0, 1, 3, 2)[i], subs)
         for e in range(2):
             arrive(e * subs + q, stage, far_fields, send_one, recv_one)
         for e in range(2):
-            place = e * subs + q
-            parts = [source_features(far_fields[place, k]) for k in range(4)]
+            for k in range(4):
+                far_feats[i % 2, e * 4 + k, :, 0:FEAT] = source_features(
+                    far_fields[e * subs + q, k]
+                )
             for x in range(2):
-                slot_at = place * 2 + x
-                target = targets[exports[x, place]]
-                pair_terms(
-                    parts[2 * x : 2 * x + 2], target, far_cubes.at[slot_at], far_dens, slot_at
-                )
-        return 0
-
-    lax.fori_loop(0, subs, far_first, 0)
+                parts = [far_feats[i % 2, e * 4 + 2 * x + k] for k in range(2)]
+                target = targets[exports[x, e * subs + q]]
+                distances(parts, target, place.at[e, pl.ds(x, 1)])
+
+    def far_drain(i, place):
+        q = lax.rem(sub + (0, 1, 3, 2)[i], subs)
+        for e in range(2):
+            for x in range(2):
+                at = (e * subs + q) * 2 + x
+                pair_terms(place.at[e, pl.ds(x, 1)], 1, far_cubes.at[at], far_dens, at)
+
+    places = (odd, even)
+    far_fill(0, places[0])
+    for i in range(1, 4):
+        far_fill(i, places[i % 2])
+        far_drain(i - 1, places[(i - 1) % 2])
+    far_drain(3, places[1])
 
     owner = lax.broadcasted_iota(jnp.int32, (BLOCKS, BLOCK), 0)
     total = near_dens[...]
@@ -299,6 +335,9 @@
     for r in range(SLOTS):
         for k in range(2):
             stage_factor[r // 2, pl.ds((r % 2) * 2 + k, 1)] = factor[pl.ds(imports[k, r], 1)]
+    second = exchange(stage_factor, far_factor, send_two, recv_two)
+    for copy in second:
+        copy.start()
     gain_all = chem_tau * (dens / (dens + 1.0))
     most = jnp.where(slot[...] >= 0, steps[...], jnp.minimum(steps[...], S_LO)).astype(F32)
     for b in range(BLOCKS // 2):
@@ -310,9 +349,6 @@
             limit[span, at] = jnp.broadcast_to(most[block : block + 1], (SPECIES, BLOCK))
     state[0:SPECIES] = species[:, 0:HALF]
     state[SPECIES : 2 * SPECIES] = species[:, HALF : 2 * HALF]
-    second = exchange(stage_factor, far_factor, send_two, recv_two)
-    for copy in second:
-        copy.start()
     part = HALF // GROUPS
     for g in range(GROUPS):
         at = pl.ds(g * part, part)
@@ -331,8 +367,8 @@
             lift = gain[:, at]
             moved = (abund + lift) + lift * jnp.tanh(rate_in[:, at])
             out = mm(left, right_side(moved))
-            rate_in[:, at] = out[2 * SPECIES :]
-            state[:, at] = jnp.where(c.astype(F32) < limit[:, at], out[: 2 * SPECIES], abund)
+            rate_in[:, at] = out[: 2 * SPECIES]
+            state[:, at] = jnp.where(c.astype(F32) < limit[:, at], out[2 * SPECIES :], abund)
 
     def with_near(i, _):
         for s in range(4):
@@ -343,38 +379,42 @@
         return 0
 
     lax.fori_loop(0, 4, with_near, 0)
+    def alone(i, _):
+        for s in range(4):
+            chem_step(16 + i * 4 + s)
+        return 0
+
+    lax.fori_loop(0, 2, alone, 0)
     for place in range(2 * subs):
         arrive(place, stage_factor, far_factor, send_two, recv_two)
     for j in range(2 * subs):
         for k in range(4):
             far_rows[j * 4 + k] = gradient_rows(far_fields[j, k], far_factor[j, k : k + 1])
-
-    def with_far(i, _):
-        for s in range(4):
-            chem_step(16 + i * 4 + s)
-            for n in range(2):
-                r = i * 8 + s * 2 + n
-                far_acc[r] = pair_sums([far_rows[r * 2 + k] for k in range(2)], far_cubes.at[r])
-        return 0
-
-    lax.fori_loop(0, 2, with_far, 0)
     row = lax.broadcasted_iota(jnp.int32, (8, BLOCK), 0)
-
-    def with_finish(i, _):
-        for s in range(4):
-            chem_step(24 + i * 4 + s)
-            for n in range(4):
-                b = i * 16 + s * 4 + n
-                acc = near_acc[b]
-                for r in range(SLOTS):
-                    acc += far_acc[r] * (exports[r % 2, r // 2] == b).astype(F32)
-                acc = acc * jnp.where(row < 4, factor[pl.ds(b, 1)], 1.0)
-                acc = acc + pltpu.roll(acc, 4, 0)
-                at = pl.ds(pl.multiple_of(b * BLOCK, BLOCK), BLOCK)
-                accel[:, at] = (4.0 * width[pl.ds(b, 1)]) * (pos[:, at] * acc[3:4] - acc[0:3])
-        return 0
-
-    lax.fori_loop(0, 2, with_finish, 0)
+    lane = lax.broadcasted_iota(jnp.int32, (8, BLOCK), 1)
+    named = jnp.zeros((8, BLOCK), jnp.int32)
+    for r in range(SLOTS):
+        named = jnp.where(lane // 8 == r, exports[r % 2, r // 2], named)
+    named = jnp.where(lane % 8 == row, named, -1)
+    for s in range(4):
+        chem_step(jnp.int32(24 + s))
+        for n in range(4):
+            r = s * 4 + n
+            far_acc[r] = pair_sums([far_rows[r * 2 + k] for k in range(2)], far_cubes.at[r])
+    pick = jnp.concatenate(
+        [jnp.where(named == b, 1.0, 0.0) for b in range(BLOCKS)], 0
+    ).astype(BF16)
+    high, low = halves(far_acc[...].reshape(SLOTS * 8, BLOCK))
+    far_all = mm(jnp.concatenate([pick, pick], 1), jnp.concatenate([high, low], 0))
+    for s in range(4):
+        chem_step(jnp.int32(28 + s))
+        for n in range(8):
+            b = s * 8 + n
+            acc = near_acc[b] + far_all[b * 8 : b * 8 + 8]
+            acc = acc * jnp.where(row < 4, factor[b : b + 1], 1.0)
+            acc = acc + pltpu.roll(acc, 4, 0)
+            at = pl.ds(b * BLOCK, BLOCK)
+            accel[:, at] = (4.0 * width[b : b + 1]) * (pos[:, at] * acc[3:4] - acc[0:3])
     abund_all[:, 0:HALF] = state[0:SPECIES]
     abund_all[:, HALF : 2 * HALF] = state[SPECIES : 2 * SPECIES]
     for copy in first + second:
@@ -437,8 +477,11 @@
         scratch_shapes=[space(x.shape, x.dtype) for space, x in zip(spaces, given)]
         + [
             pltpu.VMEM((BLOCKS, 8, BLOCK), F32),
-            pltpu.VMEM((BLOCKS, FEAT, BLOCK), BF16),
-            pltpu.VMEM((BLOCKS, BLOCK, FEAT), BF16),
+            pltpu.VMEM((BLOCKS, 2 * BLOCK, 2 * BLOCK), BF16),
+            pltpu.VMEM((BLOCKS, BLOCK, BLOCK), BF16),
+            pltpu.VMEM((2, 8, BLOCK, BLOCK), BF16),
+            pltpu.VMEM((2, NBR // 2, BLOCK, 2 * BLOCK), F32),
+            pltpu.VMEM((2, NBR // 2, BLOCK, 2 * BLOCK), F32),
             pltpu.VMEM((sides, 4, 8, BLOCK), F32),
             pltpu.VMEM((sides, 4, 8, BLOCK), F32),
             pltpu.VMEM(tile, F32),

time: 25.3 us -> 23.5 us (0.929)
  Pallas kernels: 24.6 us -> 22.7 us
    pallas_call x1, Pallas kernels: 23.8 us -> 22 us  [on_device(): pl.pallas_call(kernel, out_shape=(pltpu.VMEM(tile, F32), pltpu.VMEM(posit...]
where the time goes in v3:
time: 23.5 us; the launch traced here: 23.4 us
  Pallas kernels  22.7 us (97%)
  between operations  0.64 us (3%)
    pallas_call x1, Pallas kernels, on_device(): pl.pallas_call(kernel, out_shape=(pltpu.VMEM(tile, F32), pltpu.VMEM(posit...  22 us
    pallas_call x1, Pallas kernels, on_device(): pl.pallas_call(deliver, out_shape=(jax.ShapeDtypeStruct(tile, F32), jax.S...  0.75 us

profile of v3, /device:TPU:0, one launch (start us, length us, event | category | flops | bytes accessed | tf_op | source)
XLA Modules:
  0.0 23.4 jit_solution(6670631913633091174)
XLA Ops:
  0.6 22.0 %particle_step.1 = (f32[32,128]{1,0:T(8,128)S(1)}, f32[3,4096]{1,0:T(4,128)S(1)}, f32[12,4096]{1,0:T(8,128)S(1)}) custom-call(f32[3,4096]{1,0:T(4,128)} %pos_in.1, f32[32,128]{1,0:T(8,128)} %bitcast.9, f32[32,128]{1,0:T(8,128)} %bitcast.10, f32[32,128]{1,0:T(8,128)} %bitcast.11, f32[12,4096]{1,0:T(8,128)} %species_in.1, s32[4,32]{1,0:T(4,128)} %bitcast.14, ...), custom_call_target="tpu_custom_call" | custom-call | tf_op jit(solution)/shard_map/particle_step/pallas_call | solution.py:468
  22.6 0.7 %deliver.1 = (f32[32,128]{1,0:T(8,128)}, f32[3,4096]{1,0:T(4,128)}, f32[12,4096]{1,0:T(8,128)}) custom-call(f32[32,128]{1,0:T(8,128)S(1)} %get-tuple-element.9.density, f32[3,4096]{1,0:T(4,128)S(1)} %get-tuple-element.10.accel, f32[12,4096]{1,0:T(8,128)S(1)} %get-tuple-element.11.abund), custom_call_target="tpu_custom_call" | custom-call | tf_op jit(solution)/shard_map/deliver/pallas_call | solution.py:511

commit v4 on v3

--- a/solution.py
+++ b/solution.py
@@ -17,7 +17,7 @@
 HALF = BLOCKS * BLOCK // 2
 FEAT = 48
 GROUPS = 4
-FIRST = 8
+FIRST = 32
 MESH = pl.DeviceIdType.MESH
 F32 = jnp.float32
 BF16 = jnp.bfloat16
@@ -268,32 +268,19 @@
     left = left_side(jnp.concatenate([spread(both), jac_full], 0))
     left_first = left_side(rate_full)
 
-    def shape_more(b, _):
-        shape_block(b)
-        return 0
-
-    lax.fori_loop(FIRST, BLOCKS, shape_more, 0, unroll=4)
-
     def fill(b, place):
         distances([feats[neigh[k, b]] for k in range(NBR)], targets[b], place)
 
     def drain(b, place):
         pair_terms(place, NBR // 2, near_cubes.at[b], near_dens, b)
 
-    fill(0, even.at[0])
-    fill(1, even.at[1])
-
-    def near_first(i, _):
-        b = i * 4
-        for n in range(2):
-            fill(b + 2 + n, odd.at[n])
-            drain(b + n, even.at[n])
-        for n in range(2):
-            fill(lax.rem(b + 4 + n, BLOCKS), even.at[n])
-            drain(b + 2 + n, odd.at[n])
-        return 0
-
-    lax.fori_loop(0, BLOCKS // 4, near_first, 0)
+    ring = [even.at[0], even.at[1], odd.at[0], odd.at[1]]
+    fill(0, ring[0])
+    fill(1, ring[1])
+    for b in range(BLOCKS):
+        if b + 2 < BLOCKS:
+            fill(b + 2, ring[(b + 2) % 4])
+        drain(b, ring[b % 4])
     for name in ("energy", "steps", "slot", "species"):
         loads[name].wait()
 
@@ -368,23 +355,15 @@
             moved = (abund + lift) + lift * jnp.tanh(rate_in[:, at])
             out = mm(left, right_side(moved))
             rate_in[:, at] = out[: 2 * SPECIES]
-            state[:, at] = jnp.where(c.astype(F32) < limit[:, at], out[2 * SPECIES :], abund)
-
-    def with_near(i, _):
-        for s in range(4):
-            chem_step(i * 4 + s)
-            for n in range(2):
-                b = i * 8 + s * 2 + n
-                near_acc[b] = pair_sums([rows[neigh[k, b]] for k in range(NBR)], near_cubes.at[b])
-        return 0
-
-    lax.fori_loop(0, 4, with_near, 0)
-    def alone(i, _):
-        for s in range(4):
-            chem_step(16 + i * 4 + s)
-        return 0
-
-    lax.fori_loop(0, 2, alone, 0)
+            state[:, at] = jnp.where(limit[:, at] > c, out[2 * SPECIES :], abund)
+
+    for c in range(SMAX // 2):
+        chem_step(c)
+        for b in (2 * c, 2 * c + 1):
+            near_acc[b] = pair_sums([rows[neigh[k, b]] for k in range(NBR)], near_cubes.at[b])
+
+    for c in range(16, 24):
+        chem_step(c)
     for place in range(2 * subs):
         arrive(place, stage_factor, far_factor, send_two, recv_two)
     for j in range(2 * subs):
@@ -397,7 +376,7 @@
         named = jnp.where(lane // 8 == r, exports[r % 2, r // 2], named)
     named = jnp.where(lane % 8 == row, named, -1)
     for s in range(4):
-        chem_step(jnp.int32(24 + s))
+        chem_step(24 + s)
         for n in range(4):
             r = s * 4 + n
             far_acc[r] = pair_sums([far_rows[r * 2 + k] for k in range(2)], far_cubes.at[r])
@@ -407,7 +386,7 @@
     high, low = halves(far_acc[...].reshape(SLOTS * 8, BLOCK))
     far_all = mm(jnp.concatenate([pick, pick], 1), jnp.concatenate([high, low], 0))
     for s in range(4):
-        chem_step(jnp.int32(28 + s))
+        chem_step(28 + s)
         for n in range(8):
             b = s * 8 + n
             acc = near_acc[b] + far_all[b * 8 : b * 8 + 8]

time: 23.5 us -> 23.5 us (level)
  no operation moved by 1% of the time
where the time goes in v4:
time: 23.5 us; the launch traced here: 23.4 us
  Pallas kernels  22.7 us (97%)
  between operations  0.64 us (3%)
    pallas_call x1, Pallas kernels, on_device(): pl.pallas_call(kernel, out_shape=(pltpu.VMEM(tile, F32), pltpu.VMEM(posit...  22 us
    pallas_call x1, Pallas kernels, on_device(): pl.pallas_call(deliver, out_shape=(jax.ShapeDtypeStruct(tile, F32), jax.S...  0.75 us

profile of v4, /device:TPU:0, one launch (start us, length us, event | category | flops | bytes accessed | tf_op | source)
XLA Modules:
  0.0 23.4 jit_solution(7493404046232577130)
XLA Ops:
  0.6 22.0 %particle_step.1 = (f32[32,128]{1,0:T(8,128)S(1)}, f32[3,4096]{1,0:T(4,128)S(1)}, f32[12,4096]{1,0:T(8,128)S(1)}) custom-call(f32[3,4096]{1,0:T(4,128)} %pos_in.1, f32[32,128]{1,0:T(8,128)} %bitcast.9, f32[32,128]{1,0:T(8,128)} %bitcast.10, f32[32,128]{1,0:T(8,128)} %bitcast.11, f32[12,4096]{1,0:T(8,128)} %species_in.1, s32[4,32]{1,0:T(4,128)} %bitcast.14, ...), custom_call_target="tpu_custom_call" | custom-call | tf_op jit(solution)/shard_map/particle_step/pallas_call | solution.py:447
  22.6 0.7 %deliver.1 = (f32[32,128]{1,0:T(8,128)}, f32[3,4096]{1,0:T(4,128)}, f32[12,4096]{1,0:T(8,128)}) custom-call(f32[32,128]{1,0:T(8,128)S(1)} %get-tuple-element.9.density, f32[3,4096]{1,0:T(4,128)S(1)} %get-tuple-element.10.accel, f32[12,4096]{1,0:T(8,128)S(1)} %get-tuple-element.11.abund), custom_call_target="tpu_custom_call" | custom-call | tf_op jit(solution)/shard_map/deliver/pallas_call | solution.py:490

commit v5 on v4

--- a/solution.py
+++ b/solution.py
@@ -160,6 +160,7 @@
     recv_one,
     send_two,
     recv_two,
+    ready,
 ):
     dom = lax.axis_index("dom")
     sub = lax.axis_index("sub")
@@ -167,9 +168,14 @@
     subs = lax.axis_size("sub")
     sides = [lax.rem(dom + doms - 1, doms), lax.rem(dom + 1, doms)]
     barrier = pltpu.get_barrier_semaphore()
-    for side in sides:
+    for q in range(subs):
+        pl.semaphore_signal(barrier, inc=1, device_id=(sides[0], q), device_id_type=MESH)
+
+    @pl.when(dom != doms - 1)
+    def _():
         for q in range(subs):
-            pl.semaphore_signal(barrier, inc=1, device_id=(side, q), device_id_type=MESH)
+            pl.semaphore_signal(barrier, inc=1, device_id=(sides[1], q), device_id_type=MESH)
+
 
     pairs = {
         "pos": (pos_in, pos),
@@ -242,10 +248,22 @@
     loads["exports"].wait()
     loads["jac"].wait()
     loads["rates"].wait()
-    pl.semaphore_wait(barrier, 2 * subs)
+    pl.semaphore_wait(barrier, jnp.where(dom == 0, subs, 2 * subs))
+
+    @pl.when(dom == doms - 1)
+    def _():
+        for q in range(subs):
+            pl.semaphore_signal(ready, inc=1, device_id=(sides[1], q), device_id_type=MESH)
+
     first = exchange(stage, far_fields, send_one, recv_one)
-    for copy in first:
+    for copy in first[subs:]:
         copy.start()
+
+    @pl.when(dom != 0)
+    def _():
+        for copy in first[:subs]:
+            copy.start()
+
 
     def shape_block(b):
         place = pos[:, pl.ds(pl.multiple_of(b * BLOCK, BLOCK), BLOCK)]
@@ -283,6 +301,13 @@
         drain(b, ring[b % 4])
     for name in ("energy", "steps", "slot", "species"):
         loads[name].wait()
+
+    @pl.when(dom == 0)
+    def _():
+        pl.semaphore_wait(ready, subs)
+        for copy in first[:subs]:
+            copy.start()
+
 
     def far_fill(i, place):
         q = lax.rem(sub + (0, 1, 3, 2)[i], subs)
@@ -481,7 +506,8 @@
             pltpu.VMEM(chem, F32),
             pltpu.SemaphoreType.DMA((len(given),)),
         ]
-        + [pltpu.SemaphoreType.DMA((sides,))] * 4,
+        + [pltpu.SemaphoreType.DMA((sides,))] * 4
+        + [pltpu.SemaphoreType.REGULAR],
         compiler_params=pltpu.CompilerParams(
             collective_id=0, has_side_effects=True, vmem_limit_bytes=24 << 20
         ),

time: 23.5 us -> 25.3 us (1.077)
  Pallas kernels: 22.7 us -> 24.6 us
    pallas_call x1, Pallas kernels: 22 us -> 23.8 us  [on_device(): pl.pallas_call(kernel, out_shape=(pltpu.VMEM(tile, F32), pltpu.VMEM(posit...]
where the time goes in v5:
time: 25.3 us; the launch traced here: 25.2 us
  Pallas kernels  24.6 us (97%)
  between operations  0.64 us (3%)
    pallas_call x1, Pallas kernels, on_device(): pl.pallas_call(kernel, out_shape=(pltpu.VMEM(tile, F32), pltpu.VMEM(posit...  23.8 us
    pallas_call x1, Pallas kernels, on_device(): pl.pallas_call(deliver, out_shape=(jax.ShapeDtypeStruct(tile, F32), jax.S...  0.75 us

profile of v5, /device:TPU:0, one launch (start us, length us, event | category | flops | bytes accessed | tf_op | source)
XLA Modules:
  0.0 25.2 jit_solution(16419451819265193225)
XLA Ops:
  0.6 23.8 %particle_step.1 = (f32[32,128]{1,0:T(8,128)S(1)}, f32[3,4096]{1,0:T(4,128)S(1)}, f32[12,4096]{1,0:T(8,128)S(1)}) custom-call(f32[3,4096]{1,0:T(4,128)} %pos_in.1, f32[32,128]{1,0:T(8,128)} %bitcast.9, f32[32,128]{1,0:T(8,128)} %bitcast.10, f32[32,128]{1,0:T(8,128)} %bitcast.11, f32[12,4096]{1,0:T(8,128)} %species_in.1, s32[4,32]{1,0:T(4,128)} %bitcast.14, ...), custom_call_target="tpu_custom_call" | custom-call | tf_op jit(solution)/shard_map/particle_step/pallas_call | solution.py:472
  24.5 0.7 %deliver.1 = (f32[32,128]{1,0:T(8,128)}, f32[3,4096]{1,0:T(4,128)}, f32[12,4096]{1,0:T(8,128)}) custom-call(f32[32,128]{1,0:T(8,128)S(1)} %get-tuple-element.9.density, f32[3,4096]{1,0:T(4,128)S(1)} %get-tuple-element.10.accel, f32[12,4096]{1,0:T(8,128)S(1)} %get-tuple-element.11.abund), custom_call_target="tpu_custom_call" | custom-call | tf_op jit(solution)/shard_map/deliver/pallas_call | solution.py:516

commit v6 on v4

--- a/solution.py
+++ b/solution.py
@@ -17,6 +17,7 @@
 HALF = BLOCKS * BLOCK // 2
 FEAT = 48
 GROUPS = 4
+SPLIT = 24
 FIRST = 32
 MESH = pl.DeviceIdType.MESH
 F32 = jnp.float32
@@ -46,6 +47,13 @@
 def source_features(fields):
     high, middle, low = pieces(fields)
     return jnp.concatenate([high, high, high, middle, middle, low], 0).T.astype(BF16)
+
+
+def weighted(place, weight):
+    norm = jnp.sum(place * place, axis=0, keepdims=True)
+    return jnp.concatenate(
+        [place * weight, weight, norm * weight, jnp.zeros((3, BLOCK), F32)], 0
+    )
 
 
 def gradient_rows(fields, factor):
@@ -137,7 +145,10 @@
     far_feats,
     even,
     odd,
+    far_ring,
+    raw,
     stage,
+    far_raw,
     far_fields,
     factor,
     stage_factor,
@@ -225,25 +236,22 @@
 
     def prepare(b, _):
         place = pos[:, pl.ds(pl.multiple_of(b * BLOCK, BLOCK), BLOCK)]
-        weight = root_mass[pl.ds(b, 1)]
-        fields[b, 0:3] = place * weight
-        fields[b, 3:4] = weight
-        fields[b, 4:5] = jnp.sum(place * place, axis=0, keepdims=True) * weight
-        fields[b, 5:8] = jnp.zeros((3, BLOCK), F32)
+        raw[b, 0:3] = place
+        raw[b, 3:4] = root_mass[pl.ds(b, 1)]
         return 0
 
     lax.fori_loop(0, BLOCKS, prepare, 0, unroll=8)
     loads["imports"].wait()
     for r in range(SLOTS):
         for k in range(2):
-            stage[r // 2, (r % 2) * 2 + k] = fields[imports[k, r]]
+            stage[r // 2, (r % 2) * 2 + k] = raw[imports[k, r]]
     loads["width"].wait()
     loads["neigh"].wait()
     loads["exports"].wait()
     loads["jac"].wait()
     loads["rates"].wait()
     pl.semaphore_wait(barrier, 2 * subs)
-    first = exchange(stage, far_fields, send_one, recv_one)
+    first = exchange(stage, far_raw, send_one, recv_one)
     for copy in first:
         copy.start()
 
@@ -258,7 +266,9 @@
         split = jnp.concatenate([high, middle, low, high, middle, high], 0).astype(BF16)
         targets[b, 0:FEAT, 0:BLOCK] = split
         targets[b, BLOCK : BLOCK + FEAT, BLOCK : 2 * BLOCK] = split
-        feats[b, :, 0:FEAT] = source_features(fields[b])
+        full = weighted(place, root_mass[pl.ds(b, 1)])
+        fields[b] = full
+        feats[b, :, 0:FEAT] = source_features(full)
 
     for b in range(FIRST):
         shape_block(b)
@@ -284,33 +294,38 @@
     for name in ("energy", "steps", "slot", "species"):
         loads[name].wait()
 
-    def far_fill(i, place):
-        q = lax.rem(sub + (0, 1, 3, 2)[i], subs)
-        for e in range(2):
-            arrive(e * subs + q, stage, far_fields, send_one, recv_one)
-        for e in range(2):
-            for k in range(4):
-                far_feats[i % 2, e * 4 + k, :, 0:FEAT] = source_features(
-                    far_fields[e * subs + q, k]
-                )
-            for x in range(2):
-                parts = [far_feats[i % 2, e * 4 + 2 * x + k] for k in range(2)]
-                target = targets[exports[x, e * subs + q]]
-                distances(parts, target, place.at[e, pl.ds(x, 1)])
-
-    def far_drain(i, place):
-        q = lax.rem(sub + (0, 1, 3, 2)[i], subs)
-        for e in range(2):
-            for x in range(2):
-                at = (e * subs + q) * 2 + x
-                pair_terms(place.at[e, pl.ds(x, 1)], 1, far_cubes.at[at], far_dens, at)
-
-    places = (odd, even)
-    far_fill(0, places[0])
-    for i in range(1, 4):
-        far_fill(i, places[i % 2])
-        far_drain(i - 1, places[(i - 1) % 2])
-    far_drain(3, places[1])
+    early = jnp.where(dom == 0, 1, 0)
+    order = []
+    for e in (early, 1 - early):
+        for d in (0, 1, 3, 2):
+            order.append(e * subs + lax.rem(sub + d, subs))
+
+    def far_fill(i):
+        place = order[i]
+        for k in range(4):
+            full = weighted(far_raw[place, k, 0:3], far_raw[place, k, 3:4])
+            far_fields[place, k] = full
+            far_feats[i * 4 + k, :, 0:FEAT] = source_features(full)
+        for x in range(2):
+            parts = [far_feats[i * 4 + 2 * x + k] for k in range(2)]
+            distances(parts, targets[exports[x, place]], far_ring.at[pl.ds(2 * i + x, 1)])
+
+    def far_drain(i):
+        for x in range(2):
+            at = order[i] * 2 + x
+            pair_terms(far_ring.at[pl.ds(2 * i + x, 1)], 1, far_cubes.at[at], far_dens, at)
+
+    before = ()
+    for group in ((0, 1, 2, 3), (4, 5), (6,), (7,)):
+        for i in group:
+            arrive(order[i], stage, far_raw, send_one, recv_one)
+        for i in group:
+            far_fill(i)
+        for i in before:
+            far_drain(i)
+        before = group
+    for i in before:
+        far_drain(i)
 
     owner = lax.broadcasted_iota(jnp.int32, (BLOCKS, BLOCK), 0)
     total = near_dens[...]
@@ -362,38 +377,52 @@
         for b in (2 * c, 2 * c + 1):
             near_acc[b] = pair_sums([rows[neigh[k, b]] for k in range(NBR)], near_cubes.at[b])
 
-    for c in range(16, 24):
-        chem_step(c)
-    for place in range(2 * subs):
-        arrive(place, stage_factor, far_factor, send_two, recv_two)
-    for j in range(2 * subs):
-        for k in range(4):
-            far_rows[j * 4 + k] = gradient_rows(far_fields[j, k], far_factor[j, k : k + 1])
     row = lax.broadcasted_iota(jnp.int32, (8, BLOCK), 0)
     lane = lax.broadcasted_iota(jnp.int32, (8, BLOCK), 1)
     named = jnp.zeros((8, BLOCK), jnp.int32)
     for r in range(SLOTS):
         named = jnp.where(lane // 8 == r, exports[r % 2, r // 2], named)
     named = jnp.where(lane % 8 == row, named, -1)
-    for s in range(4):
-        chem_step(24 + s)
-        for n in range(4):
-            r = s * 4 + n
-            far_acc[r] = pair_sums([far_rows[r * 2 + k] for k in range(2)], far_cubes.at[r])
     pick = jnp.concatenate(
         [jnp.where(named == b, 1.0, 0.0) for b in range(BLOCKS)], 0
     ).astype(BF16)
+    for c in range(16, SPLIT):
+        chem_step(c)
+
+    def rows_far(group):
+        for i in group:
+            arrive(order[i], stage_factor, far_factor, send_two, recv_two)
+        for i in group:
+            place = order[i]
+            for k in range(4):
+                far_rows[i * 4 + k] = gradient_rows(
+                    far_fields[place, k], far_factor[place, pl.ds(k, 1)]
+                )
+
+    def sums_far(i, x):
+        at = order[i] * 2 + x
+        parts = [far_rows[i * 4 + 2 * x + k] for k in range(2)]
+        far_acc[at] = pair_sums(parts, far_cubes.at[at])
+
+    rows_far((0, 1, 2, 3))
+    slots = [(i, x) for i in range(4) for x in range(2)]
+    for c in range(SPLIT, SMAX):
+        chem_step(c)
+        n = 8 // (SMAX - SPLIT)
+        for i, x in slots[(c - SPLIT) * n : (c - SPLIT + 1) * n]:
+            sums_far(i, x)
+    rows_far((4, 5, 6, 7))
+    for i in range(4, 8):
+        for x in range(2):
+            sums_far(i, x)
     high, low = halves(far_acc[...].reshape(SLOTS * 8, BLOCK))
     far_all = mm(jnp.concatenate([pick, pick], 1), jnp.concatenate([high, low], 0))
-    for s in range(4):
-        chem_step(28 + s)
-        for n in range(8):
-            b = s * 8 + n
-            acc = near_acc[b] + far_all[b * 8 : b * 8 + 8]
-            acc = acc * jnp.where(row < 4, factor[b : b + 1], 1.0)
-            acc = acc + pltpu.roll(acc, 4, 0)
-            at = pl.ds(b * BLOCK, BLOCK)
-            accel[:, at] = (4.0 * width[b : b + 1]) * (pos[:, at] * acc[3:4] - acc[0:3])
+    for b in range(BLOCKS):
+        acc = near_acc[b] + far_all[b * 8 : b * 8 + 8]
+        acc = acc * jnp.where(row < 4, factor[b : b + 1], 1.0)
+        acc = acc + pltpu.roll(acc, 4, 0)
+        at = pl.ds(b * BLOCK, BLOCK)
+        accel[:, at] = (4.0 * width[b : b + 1]) * (pos[:, at] * acc[3:4] - acc[0:3])
     abund_all[:, 0:HALF] = state[0:SPECIES]
     abund_all[:, HALF : 2 * HALF] = state[SPECIES : 2 * SPECIES]
     for copy in first + second:
@@ -458,10 +487,13 @@
             pltpu.VMEM((BLOCKS, 8, BLOCK), F32),
             pltpu.VMEM((BLOCKS, 2 * BLOCK, 2 * BLOCK), BF16),
             pltpu.VMEM((BLOCKS, BLOCK, BLOCK), BF16),
-            pltpu.VMEM((2, 8, BLOCK, BLOCK), BF16),
+            pltpu.VMEM((far, BLOCK, BLOCK), BF16),
             pltpu.VMEM((2, NBR // 2, BLOCK, 2 * BLOCK), F32),
             pltpu.VMEM((2, NBR // 2, BLOCK, 2 * BLOCK), F32),
-            pltpu.VMEM((sides, 4, 8, BLOCK), F32),
+            pltpu.VMEM((SLOTS, BLOCK, 2 * BLOCK), F32),
+            pltpu.VMEM((BLOCKS, 4, BLOCK), F32),
+            pltpu.VMEM((sides, 4, 4, BLOCK), F32),
+            pltpu.VMEM((sides, 4, 4, BLOCK), F32),
             pltpu.VMEM((sides, 4, 8, BLOCK), F32),
             pltpu.VMEM(tile, F32),
             pltpu.VMEM((sides, 4, BLOCK), F32),

time: 23.5 us -> 22.2 us (0.945)
  Pallas kernels: 22.7 us -> 21.4 us
    pallas_call x1, Pallas kernels: 22 us -> 20.7 us  [on_device(): pl.pallas_call(kernel, out_shape=(pltpu.VMEM(tile, F32), pltpu.VMEM(posit...]
where the time goes in v6:
time: 22.2 us; the launch traced here: 22 us
  Pallas kernels  21.4 us (96%)
  between operations  0.64 us (3%)
    pallas_call x1, Pallas kernels, on_device(): pl.pallas_call(kernel, out_shape=(pltpu.VMEM(tile, F32), pltpu.VMEM(posit...  20.7 us
    pallas_call x1, Pallas kernels, on_device(): pl.pallas_call(deliver, out_shape=(jax.ShapeDtypeStruct(tile, F32), jax.S...  0.75 us

profile of v6, /device:TPU:0, one launch (start us, length us, event | category | flops | bytes accessed | tf_op | source)
XLA Modules:
  0.0 22.0 jit_solution(11200117465250334148)
XLA Ops:
  0.6 20.7 %particle_step.1 = (f32[32,128]{1,0:T(8,128)S(1)}, f32[3,4096]{1,0:T(4,128)S(1)}, f32[12,4096]{1,0:T(8,128)S(1)}) custom-call(f32[3,4096]{1,0:T(4,128)} %pos_in.1, f32[32,128]{1,0:T(8,128)} %bitcast.9, f32[32,128]{1,0:T(8,128)} %bitcast.10, f32[32,128]{1,0:T(8,128)} %bitcast.11, f32[12,4096]{1,0:T(8,128)} %species_in.1, s32[4,32]{1,0:T(4,128)} %bitcast.14, ...), custom_call_target="tpu_custom_call" | custom-call | tf_op jit(solution)/shard_map/particle_step/pallas_call | solution.py:476
  21.3 0.7 %deliver.1 = (f32[32,128]{1,0:T(8,128)}, f32[3,4096]{1,0:T(4,128)}, f32[12,4096]{1,0:T(8,128)}) custom-call(f32[32,128]{1,0:T(8,128)S(1)} %get-tuple-element.9.density, f32[3,4096]{1,0:T(4,128)S(1)} %get-tuple-element.10.accel, f32[12,4096]{1,0:T(8,128)S(1)} %get-tuple-element.11.abund), custom_call_target="tpu_custom_call" | custom-call | tf_op jit(solution)/shard_map/deliver/pallas_call | solution.py:522

commit v7 on v6

--- a/solution.py
+++ b/solution.py
@@ -294,7 +294,7 @@
     for name in ("energy", "steps", "slot", "species"):
         loads[name].wait()
 
-    early = jnp.where(dom == 0, 1, 0)
+    early = jnp.where(dom < doms // 2, 1, 0)
     order = []
     for e in (early, 1 - early):
         for d in (0, 1, 3, 2):
@@ -312,8 +312,8 @@
 
     def far_drain(i):
         for x in range(2):
-            at = order[i] * 2 + x
-            pair_terms(far_ring.at[pl.ds(2 * i + x, 1)], 1, far_cubes.at[at], far_dens, at)
+            at = 2 * i + x
+            pair_terms(far_ring.at[pl.ds(at, 1)], 1, far_cubes.at[at], far_dens, at)
 
     before = ()
     for group in ((0, 1, 2, 3), (4, 5), (6,), (7,)):
@@ -330,7 +330,7 @@
     owner = lax.broadcasted_iota(jnp.int32, (BLOCKS, BLOCK), 0)
     total = near_dens[...]
     for r in range(SLOTS):
-        total += jnp.where(owner == exports[r % 2, r // 2], far_dens[r : r + 1], 0.0)
+        total += jnp.where(owner == exports[r % 2, order[r // 2]], far_dens[r : r + 1], 0.0)
     dens = total * width[...]
     density[...] = dens
     factor[...] = (gamma_gas - 1.0) * energy[...] / dens
@@ -338,7 +338,7 @@
         for k in range(2):
             stage_factor[r // 2, pl.ds((r % 2) * 2 + k, 1)] = factor[pl.ds(imports[k, r], 1)]
     second = exchange(stage_factor, far_factor, send_two, recv_two)
-    for copy in second:
+    for copy in second[subs:] + second[:subs]:
         copy.start()
     gain_all = chem_tau * (dens / (dens + 1.0))
     most = jnp.where(slot[...] >= 0, steps[...], jnp.minimum(steps[...], S_LO)).astype(F32)
@@ -381,7 +381,7 @@
     lane = lax.broadcasted_iota(jnp.int32, (8, BLOCK), 1)
     named = jnp.zeros((8, BLOCK), jnp.int32)
     for r in range(SLOTS):
-        named = jnp.where(lane // 8 == r, exports[r % 2, r // 2], named)
+        named = jnp.where(lane // 8 == r, exports[r % 2, order[r // 2]], named)
     named = jnp.where(lane % 8 == row, named, -1)
     pick = jnp.concatenate(
         [jnp.where(named == b, 1.0, 0.0) for b in range(BLOCKS)], 0
@@ -400,7 +400,7 @@
                 )
 
     def sums_far(i, x):
-        at = order[i] * 2 + x
+        at = 2 * i + x
         parts = [far_rows[i * 4 + 2 * x + k] for k in range(2)]
         far_acc[at] = pair_sums(parts, far_cubes.at[at])
 
@@ -411,10 +411,11 @@
         n = 8 // (SMAX - SPLIT)
         for i, x in slots[(c - SPLIT) * n : (c - SPLIT + 1) * n]:
             sums_far(i, x)
-    rows_far((4, 5, 6, 7))
-    for i in range(4, 8):
-        for x in range(2):
-            sums_far(i, x)
+    for group in ((4, 5), (6,), (7,)):
+        rows_far(group)
+        for i in group:
+            for x in range(2):
+                sums_far(i, x)
     high, low = halves(far_acc[...].reshape(SLOTS * 8, BLOCK))
     far_all = mm(jnp.concatenate([pick, pick], 1), jnp.concatenate([high, low], 0))
     for b in range(BLOCKS):

time: 22.2 us -> 22.2 us (level)
  no operation moved by 1% of the time
where the time goes in v7:
time: 22.2 us; the launch traced here: 22.1 us
  Pallas kernels  21.4 us (96%)
  between operations  0.64 us (3%)
    pallas_call x1, Pallas kernels, on_device(): pl.pallas_call(kernel, out_shape=(pltpu.VMEM(tile, F32), pltpu.VMEM(posit...  20.7 us
    pallas_call x1, Pallas kernels, on_device(): pl.pallas_call(deliver, out_shape=(jax.ShapeDtypeStruct(tile, F32), jax.S...  0.75 us

profile of v7, /device:TPU:0, one launch (start us, length us, event | category | flops | bytes accessed | tf_op | source)
XLA Modules:
  0.0 22.1 jit_solution(9825375468887555745)
XLA Ops:
  0.6 20.7 %particle_step.1 = (f32[32,128]{1,0:T(8,128)S(1)}, f32[3,4096]{1,0:T(4,128)S(1)}, f32[12,4096]{1,0:T(8,128)S(1)}) custom-call(f32[3,4096]{1,0:T(4,128)} %pos_in.1, f32[32,128]{1,0:T(8,128)} %bitcast.9, f32[32,128]{1,0:T(8,128)} %bitcast.10, f32[32,128]{1,0:T(8,128)} %bitcast.11, f32[12,4096]{1,0:T(8,128)} %species_in.1, s32[4,32]{1,0:T(4,128)} %bitcast.14, ...), custom_call_target="tpu_custom_call" | custom-call | tf_op jit(solution)/shard_map/particle_step/pallas_call | solution.py:477
  21.3 0.7 %deliver.1 = (f32[32,128]{1,0:T(8,128)}, f32[3,4096]{1,0:T(4,128)}, f32[12,4096]{1,0:T(8,128)}) custom-call(f32[32,128]{1,0:T(8,128)S(1)} %get-tuple-element.9.density, f32[3,4096]{1,0:T(4,128)S(1)} %get-tuple-element.10.accel, f32[12,4096]{1,0:T(8,128)S(1)} %get-tuple-element.11.abund), custom_call_target="tpu_custom_call" | custom-call | tf_op jit(solution)/shard_map/deliver/pallas_call | solution.py:523

commit v8 on v7

--- a/solution.py
+++ b/solution.py
@@ -171,6 +171,12 @@
     recv_one,
     send_two,
     recv_two,
+    relay,
+    send_mate,
+    recv_mate,
+    send_wrap,
+    recv_wrap,
+    ready,
 ):
     dom = lax.axis_index("dom")
     sub = lax.axis_index("sub")
@@ -178,9 +184,27 @@
     subs = lax.axis_size("sub")
     sides = [lax.rem(dom + doms - 1, doms), lax.rem(dom + 1, doms)]
     barrier = pltpu.get_barrier_semaphore()
-    for side in sides:
+    last = doms - 1
+    for q in range(subs):
+        pl.semaphore_signal(barrier, inc=1, device_id=(sides[0], q), device_id_type=MESH)
+
+    @pl.when(dom < last - 1)
+    def _():
         for q in range(subs):
-            pl.semaphore_signal(barrier, inc=1, device_id=(side, q), device_id_type=MESH)
+            pl.semaphore_signal(barrier, inc=1, device_id=(sides[1], q), device_id_type=MESH)
+
+    mates = [lax.rem(sub + k, subs) for k in range(1, subs)]
+
+    @pl.when(dom == 0)
+    def _():
+        for q in mates:
+            pl.semaphore_signal(barrier, inc=1, device_id=(dom, q), device_id_type=MESH)
+
+    @pl.when(dom == last)
+    def _():
+        pl.semaphore_wait(barrier, subs)
+        pl.semaphore_signal(ready, inc=1, device_id=(sides[1], sub), device_id_type=MESH)
+
 
     pairs = {
         "pos": (pos_in, pos),
@@ -250,10 +274,50 @@
     loads["exports"].wait()
     loads["jac"].wait()
     loads["rates"].wait()
-    pl.semaphore_wait(barrier, 2 * subs)
     first = exchange(stage, far_raw, send_one, recv_one)
-    for copy in first:
+    relayed = [
+        pltpu.make_async_remote_copy(
+            src_ref=stage.at[q],
+            dst_ref=relay.at[sub],
+            send_sem=send_mate.at[k],
+            recv_sem=recv_mate.at[k],
+            device_id=(dom, q),
+            device_id_type=MESH,
+        )
+        for k, q in enumerate(mates)
+    ]
+    wrapped = pltpu.make_async_remote_copy(
+        src_ref=relay,
+        dst_ref=far_raw.at[pl.ds(subs, subs)],
+        send_sem=send_wrap,
+        recv_sem=recv_wrap,
+        device_id=(sides[0], sub),
+        device_id_type=MESH,
+    )
+
+    @pl.when(dom != last)
+    def _():
+        pl.semaphore_wait(barrier, jnp.where(dom == 0, 2 * subs - 1, 2 * subs))
+
+    @pl.when(dom == last - 1)
+    def _():
+        for q in range(subs):
+            pl.semaphore_signal(ready, inc=1, device_id=(sides[1], q), device_id_type=MESH)
+
+    for copy in first[subs:]:
         copy.start()
+
+    @pl.when((dom != 0) & (dom != last))
+    def _():
+        for copy in first[:subs]:
+            copy.start()
+
+    @pl.when(dom == 0)
+    def _():
+        for copy in relayed:
+            copy.start()
+        relay[sub] = stage[sub]
+
 
     def shape_block(b):
         place = pos[:, pl.ds(pl.multiple_of(b * BLOCK, BLOCK), BLOCK)]
@@ -294,6 +358,27 @@
     for name in ("energy", "steps", "slot", "species"):
         loads[name].wait()
 
+    @pl.when(dom == 0)
+    def _():
+        for k in range(subs - 1):
+            pltpu.make_async_remote_copy(
+                src_ref=stage.at[0],
+                dst_ref=relay.at[lax.rem(sub + subs - 1 - k, subs)],
+                send_sem=send_mate.at[k],
+                recv_sem=recv_mate.at[k],
+                device_id=(dom, mates[k]),
+                device_id_type=MESH,
+            ).wait_recv()
+        pl.semaphore_wait(ready, 1)
+        wrapped.start()
+
+    @pl.when(dom == last)
+    def _():
+        pl.semaphore_wait(ready, subs)
+        for copy in first[:subs]:
+            copy.start()
+
+
     early = jnp.where(dom < doms // 2, 1, 0)
     order = []
     for e in (early, 1 - early):
@@ -317,8 +402,22 @@
 
     before = ()
     for group in ((0, 1, 2, 3), (4, 5), (6,), (7,)):
-        for i in group:
-            arrive(order[i], stage, far_raw, send_one, recv_one)
+        if group[0] < subs:
+            for i in group:
+                arrive(order[i], stage, far_raw, send_one, recv_one)
+        else:
+
+            @pl.when(dom != last)
+            def _():
+                for i in group:
+                    arrive(order[i], stage, far_raw, send_one, recv_one)
+
+            if group[0] == subs:
+
+                @pl.when(dom == last)
+                def _():
+                    wrapped.wait_recv()
+
         for i in group:
             far_fill(i)
         for i in before:
@@ -426,8 +525,18 @@
         accel[:, at] = (4.0 * width[b : b + 1]) * (pos[:, at] * acc[3:4] - acc[0:3])
     abund_all[:, 0:HALF] = state[0:SPECIES]
     abund_all[:, HALF : 2 * HALF] = state[SPECIES : 2 * SPECIES]
-    for copy in first + second:
+    for copy in first[subs:] + second:
         copy.wait_send()
+
+    @pl.when(dom != 0)
+    def _():
+        for copy in first[:subs]:
+            copy.wait_send()
+
+    @pl.when(dom == 0)
+    def _():
+        for copy in relayed + [wrapped]:
+            copy.wait_send()
 
 
 def deliver(density, accel, abund, dens_out, accel_out, abund_out, sems):
@@ -514,7 +623,15 @@
             pltpu.VMEM(chem, F32),
             pltpu.SemaphoreType.DMA((len(given),)),
         ]
-        + [pltpu.SemaphoreType.DMA((sides,))] * 4,
+        + [pltpu.SemaphoreType.DMA((sides,))] * 4
+        + [
+            pltpu.VMEM((4, 4, 4, BLOCK), F32),
+            pltpu.SemaphoreType.DMA((3,)),
+            pltpu.SemaphoreType.DMA((3,)),
+            pltpu.SemaphoreType.DMA,
+            pltpu.SemaphoreType.DMA,
+            pltpu.SemaphoreType.REGULAR,
+        ],
         compiler_params=pltpu.CompilerParams(
             collective_id=0, has_side_effects=True, vmem_limit_bytes=24 << 20
         ),

time: 22.2 us -> 20.1 us (0.905)
  Pallas kernels: 21.4 us -> 19.3 us
    pallas_call x1, Pallas kernels: 20.7 us -> 18.6 us  [on_device(): pl.pallas_call(kernel, out_shape=(pltpu.VMEM(tile, F32), pltpu.VMEM(posit...]
where the time goes in v8:
time: 20.1 us; the launch traced here: 20 us
  Pallas kernels  19.3 us (96%)
  between operations  0.64 us (3%)
    pallas_call x1, Pallas kernels, on_device(): pl.pallas_call(kernel, out_shape=(pltpu.VMEM(tile, F32), pltpu.VMEM(posit...  18.6 us
    pallas_call x1, Pallas kernels, on_device(): pl.pallas_call(deliver, out_shape=(jax.ShapeDtypeStruct(tile, F32), jax.S...  0.75 us

profile of v8, /device:TPU:0, one launch (start us, length us, event | category | flops | bytes accessed | tf_op | source)
XLA Modules:
  0.0 20.0 jit_solution(3110352972712716230)
XLA Ops:
  0.6 18.6 %particle_step.1 = (f32[32,128]{1,0:T(8,128)S(1)}, f32[3,4096]{1,0:T(4,128)S(1)}, f32[12,4096]{1,0:T(8,128)S(1)}) custom-call(f32[3,4096]{1,0:T(4,128)} %pos_in.1, f32[32,128]{1,0:T(8,128)} %bitcast.9, f32[32,128]{1,0:T(8,128)} %bitcast.10, f32[32,128]{1,0:T(8,128)} %bitcast.11, f32[12,4096]{1,0:T(8,128)} %species_in.1, s32[4,32]{1,0:T(4,128)} %bitcast.14, ...), custom_call_target="tpu_custom_call" | custom-call | tf_op jit(solution)/shard_map/particle_step/pallas_call | solution.py:586
  19.2 0.7 %deliver.1 = (f32[32,128]{1,0:T(8,128)}, f32[3,4096]{1,0:T(4,128)}, f32[12,4096]{1,0:T(8,128)}) custom-call(f32[32,128]{1,0:T(8,128)S(1)} %get-tuple-element.9.density, f32[3,4096]{1,0:T(4,128)S(1)} %get-tuple-element.10.accel, f32[12,4096]{1,0:T(8,128)S(1)} %get-tuple-element.11.abund), custom_call_target="tpu_custom_call" | custom-call | tf_op jit(solution)/shard_map/deliver/pallas_call | solution.py:640

commit v9 on v8

--- a/solution.py
+++ b/solution.py
@@ -379,7 +379,7 @@
             copy.start()
 
 
-    early = jnp.where(dom < doms // 2, 1, 0)
+    early = jnp.where(dom == 1, 1, 1 - lax.rem(dom, 2))
     order = []
     for e in (early, 1 - early):
         for d in (0, 1, 3, 2):

time: 20.1 us -> 20.1 us (level)
  no operation moved by 1% of the time
where the time goes in v9:
time: 20.1 us; the launch traced here: 20 us
  Pallas kernels  19.3 us (96%)
  between operations  0.64 us (3%)
    pallas_call x1, Pallas kernels, on_device(): pl.pallas_call(kernel, out_shape=(pltpu.VMEM(tile, F32), pltpu.VMEM(posit...  18.6 us
    pallas_call x1, Pallas kernels, on_device(): pl.pallas_call(deliver, out_shape=(jax.ShapeDtypeStruct(tile, F32), jax.S...  0.75 us

profile of v9, /device:TPU:0, one launch (start us, length us, event | category | flops | bytes accessed | tf_op | source)
XLA Modules:
  0.0 20.0 jit_solution(17347450537649399975)
XLA Ops:
  0.6 18.6 %particle_step.1 = (f32[32,128]{1,0:T(8,128)S(1)}, f32[3,4096]{1,0:T(4,128)S(1)}, f32[12,4096]{1,0:T(8,128)S(1)}) custom-call(f32[3,4096]{1,0:T(4,128)} %pos_in.1, f32[32,128]{1,0:T(8,128)} %bitcast.9, f32[32,128]{1,0:T(8,128)} %bitcast.10, f32[32,128]{1,0:T(8,128)} %bitcast.11, f32[12,4096]{1,0:T(8,128)} %species_in.1, s32[4,32]{1,0:T(4,128)} %bitcast.14, ...), custom_call_target="tpu_custom_call" | custom-call | tf_op jit(solution)/shard_map/particle_step/pallas_call | solution.py:586
  19.2 0.7 %deliver.1 = (f32[32,128]{1,0:T(8,128)}, f32[3,4096]{1,0:T(4,128)}, f32[12,4096]{1,0:T(8,128)}) custom-call(f32[32,128]{1,0:T(8,128)S(1)} %get-tuple-element.9.density, f32[3,4096]{1,0:T(4,128)S(1)} %get-tuple-element.10.accel, f32[12,4096]{1,0:T(8,128)S(1)} %get-tuple-element.11.abund), custom_call_target="tpu_custom_call" | custom-call | tf_op jit(solution)/shard_map/deliver/pallas_call | solution.py:640

commit v10 on v9

--- a/solution.py
+++ b/solution.py
@@ -269,11 +269,6 @@
     for r in range(SLOTS):
         for k in range(2):
             stage[r // 2, (r % 2) * 2 + k] = raw[imports[k, r]]
-    loads["width"].wait()
-    loads["neigh"].wait()
-    loads["exports"].wait()
-    loads["jac"].wait()
-    loads["rates"].wait()
     first = exchange(stage, far_raw, send_one, recv_one)
     relayed = [
         pltpu.make_async_remote_copy(
@@ -318,6 +313,12 @@
             copy.start()
         relay[sub] = stage[sub]
 
+
+    loads["width"].wait()
+    loads["neigh"].wait()
+    loads["exports"].wait()
+    loads["jac"].wait()
+    loads["rates"].wait()
 
     def shape_block(b):
         place = pos[:, pl.ds(pl.multiple_of(b * BLOCK, BLOCK), BLOCK)]
@@ -510,7 +511,9 @@
         n = 8 // (SMAX - SPLIT)
         for i, x in slots[(c - SPLIT) * n : (c - SPLIT + 1) * n]:
             sums_far(i, x)
-    for group in ((4, 5), (6,), (7,)):
+    abund_all[:, 0:HALF] = state[0:SPECIES]
+    abund_all[:, HALF : 2 * HALF] = state[SPECIES : 2 * SPECIES]
+    for group in ((4, 5), (6, 7)):
         rows_far(group)
         for i in group:
             for x in range(2):
@@ -523,8 +526,6 @@
         acc = acc + pltpu.roll(acc, 4, 0)
         at = pl.ds(b * BLOCK, BLOCK)
         accel[:, at] = (4.0 * width[b : b + 1]) * (pos[:, at] * acc[3:4] - acc[0:3])
-    abund_all[:, 0:HALF] = state[0:SPECIES]
-    abund_all[:, HALF : 2 * HALF] = state[SPECIES : 2 * SPECIES]
     for copy in first[subs:] + second:
         copy.wait_send()
 

time: 20.1 us -> 20.1 us (level)
  no operation moved by 1% of the time
where the time goes in v10:
time: 20.1 us; the launch traced here: 20 us
  Pallas kernels  19.3 us (96%)
  between operations  0.64 us (3%)
    pallas_call x1, Pallas kernels, on_device(): pl.pallas_call(kernel, out_shape=(pltpu.VMEM(tile, F32), pltpu.VMEM(posit...  18.6 us
    pallas_call x1, Pallas kernels, on_device(): pl.pallas_call(deliver, out_shape=(jax.ShapeDtypeStruct(tile, F32), jax.S...  0.75 us

profile of v10, /device:TPU:0, one launch (start us, length us, event | category | flops | bytes accessed | tf_op | source)
XLA Modules:
  0.0 20.0 jit_solution(10287775578058892316)
XLA Ops:
  0.6 18.6 %particle_step.1 = (f32[32,128]{1,0:T(8,128)S(1)}, f32[3,4096]{1,0:T(4,128)S(1)}, f32[12,4096]{1,0:T(8,128)S(1)}) custom-call(f32[3,4096]{1,0:T(4,128)} %pos_in.1, f32[32,128]{1,0:T(8,128)} %bitcast.9, f32[32,128]{1,0:T(8,128)} %bitcast.10, f32[32,128]{1,0:T(8,128)} %bitcast.11, f32[12,4096]{1,0:T(8,128)} %species_in.1, s32[4,32]{1,0:T(4,128)} %bitcast.14, ...), custom_call_target="tpu_custom_call" | custom-call | tf_op jit(solution)/shard_map/particle_step/pallas_call | solution.py:587
  19.2 0.7 %deliver.1 = (f32[32,128]{1,0:T(8,128)}, f32[3,4096]{1,0:T(4,128)}, f32[12,4096]{1,0:T(8,128)}) custom-call(f32[32,128]{1,0:T(8,128)S(1)} %get-tuple-element.9.density, f32[3,4096]{1,0:T(4,128)S(1)} %get-tuple-element.10.accel, f32[12,4096]{1,0:T(8,128)S(1)} %get-tuple-element.11.abund), custom_call_target="tpu_custom_call" | custom-call | tf_op jit(solution)/shard_map/deliver/pallas_call | solution.py:641

commit v11 on v8

--- a/solution.py
+++ b/solution.py
@@ -16,7 +16,7 @@
 SMAX = 32
 HALF = BLOCKS * BLOCK // 2
 FEAT = 48
-GROUPS = 4
+GROUPS = 2
 SPLIT = 24
 FIRST = 32
 MESH = pl.DeviceIdType.MESH

time: 20.1 us -> 20.1 us (level)
  no operation moved by 1% of the time
where the time goes in v11:
time: 20.1 us; the launch traced here: 20 us
  Pallas kernels  19.3 us (96%)
  between operations  0.64 us (3%)
    pallas_call x1, Pallas kernels, on_device(): pl.pallas_call(kernel, out_shape=(pltpu.VMEM(tile, F32), pltpu.VMEM(posit...  18.6 us
    pallas_call x1, Pallas kernels, on_device(): pl.pallas_call(deliver, out_shape=(jax.ShapeDtypeStruct(tile, F32), jax.S...  0.75 us

profile of v11, /device:TPU:0, one launch (start us, length us, event | category | flops | bytes accessed | tf_op | source)
XLA Modules:
  0.0 20.0 jit_solution(3110352972712716230)
XLA Ops:
  0.6 18.6 %particle_step.1 = (f32[32,128]{1,0:T(8,128)S(1)}, f32[3,4096]{1,0:T(4,128)S(1)}, f32[12,4096]{1,0:T(8,128)S(1)}) custom-call(f32[3,4096]{1,0:T(4,128)} %pos_in.1, f32[32,128]{1,0:T(8,128)} %bitcast.9, f32[32,128]{1,0:T(8,128)} %bitcast.10, f32[32,128]{1,0:T(8,128)} %bitcast.11, f32[12,4096]{1,0:T(8,128)} %species_in.1, s32[4,32]{1,0:T(4,128)} %bitcast.14, ...), custom_call_target="tpu_custom_call" | custom-call | tf_op jit(solution)/shard_map/particle_step/pallas_call | solution.py:586
  19.2 0.7 %deliver.1 = (f32[32,128]{1,0:T(8,128)}, f32[3,4096]{1,0:T(4,128)}, f32[12,4096]{1,0:T(8,128)}) custom-call(f32[32,128]{1,0:T(8,128)S(1)} %get-tuple-element.9.density, f32[3,4096]{1,0:T(4,128)S(1)} %get-tuple-element.10.accel, f32[12,4096]{1,0:T(8,128)S(1)} %get-tuple-element.11.abund), custom_call_target="tpu_custom_call" | custom-call | tf_op jit(solution)/shard_map/deliver/pallas_call | solution.py:640
